TPU v7x, 256 devices: a whole 4x4x8 slice. The times are simulated.
256 devices in a mesh: row: 8 (over z_lo, x), col: 32 (over z_hi, y, core).
Axes of the slice: x: 4, y: 4, z: 8 (z_hi: 4, z_lo: 2; z = z_hi * 2 + z_lo), core: 2. Of those that a mesh axis runs over, the one named last changes fastest.
Arguments:
- wave_field: float32 [64, 128, 64, 128], P(None, 'col', 'row'), may hold values from -6 to 6
- medium_term: float32 [128, 64, 128], P('col', 'row'), may hold values from 0.5 to 4
- node_flux: float32 [64, 32, 8, 384], P(None, 'col', 'row'), may hold values from -6 to 6
- node_cell: int32 [32, 8, 384], P('col', 'row'), may hold values from 0 to 4095
- block_target: int32 [32, 8, 32], P('col', 'row'), may hold values from 0 to 31, as said below
- boundary_matrix: bfloat16 [2, 4096, 98304], P(None, 'row', 'col'), may hold values from -0.0390625 to 0.0390625
Outputs:
- volume_image: float32 [64, 128, 64, 128], P(None, 'col', 'row')
- boundary_image: float32 [4096, 64], P(('row', 'col'))
Inputs may be any that keep to these rules, and one draw needn't show every extreme that they name: For every brick (c, r), block_target[c, r, :] is a permutation of the 32 column blocks.
All inputs are finite; a program needn't handle non-finite values.
Results may differ from a plain program's by a relative error of at most 0.0029.
Values may be sent and summed in bfloat16 or wider, within the bound.
A program may use at most 64 MiB of HBM per device.

v0:
```python
import jax
import jax.numpy as jnp
from jax import lax
from jax.sharding import PartitionSpec as P


def in_order(tiles, dim):
    tiles = jnp.moveaxis(tiles, 0, dim)
    lengths = tiles.shape
    return tiles.reshape(*lengths[:dim], lengths[dim] * lengths[dim + 1], *lengths[dim + 2 :])


def sent_to_all(x, axis):
    count = lax.axis_size(axis)
    return lax.all_to_all(jnp.broadcast_to(x[None], (count, *x.shape)), axis, 0, 0, tiled=True)


def gather_directly(x, axis, dim):
    return in_order(sent_to_all(x, axis), dim)


def padded_2(block, sides, width):
    for axis, dim in sides:
        count = lax.axis_size(axis)
        forward = [(i, i + 1) for i in range(count - 1)]
        backward = [(target, source) for source, target in forward]
        low = lax.ppermute(
            lax.slice_in_dim(block, block.shape[dim] - width, None, axis=dim), axis, forward
        )
        high = lax.ppermute(lax.slice_in_dim(block, 0, width, axis=dim), axis, backward)
        block = jnp.concatenate([low, block, high], axis=dim)
    return block


def in_blocks(x, dim, count):
    lengths = x.shape
    tiles = x.reshape(*lengths[:dim], count, lengths[dim] // count, *lengths[dim + 1 :])
    return jnp.moveaxis(tiles, dim, 0)


def sum_at_owner(x, axis, dim):
    count = lax.axis_size(axis)
    tiles = lax.all_to_all(in_blocks(x, dim, count), axis, 0, 0, tiled=True)
    return jnp.sum(tiles, axis=0)


def three_tap(values, axis, side_weight, centre_weight):
    length = values.shape[axis]
    lower = lax.slice_in_dim(values, 0, length - 2, axis=axis)
    middle = lax.slice_in_dim(values, 1, length - 1, axis=axis)
    upper = lax.slice_in_dim(values, 2, length, axis=axis)
    return side_weight * (lower + upper) + centre_weight * middle


def on_device(wave_field, medium_term, node_flux, node_cell, block_target, boundary_matrix):
    components, width_x, width_y, depth_cells = wave_field.shape
    cell_total = width_x * width_y * depth_cells
    angles = components // 2
    col_count = lax.axis_size("col")
    node_total = node_cell.shape[-1]
    slot_len = node_total // col_count
    targets = block_target.reshape(col_count)
    block_ids = jnp.arange(col_count, dtype=jnp.int32)
    matches = targets[None, :] == block_ids[:, None]
    slot_cells = node_cell.reshape(col_count, slot_len)
    ordered = jnp.sum(jnp.where(matches[:, :, None], slot_cells[None, :, :], 0), axis=1).reshape(
        node_total
    )
    flat_field = wave_field.reshape(components, cell_total)
    traces = jnp.take(flat_field, ordered, axis=1).astype(jnp.bfloat16)
    received = lax.all_to_all(traces, "col", split_axis=1, concat_axis=1, tiled=True)
    column_traces = gather_directly(received, "row", 1)
    padded = padded_2(wave_field, (("row", 2), ("col", 1)), 1)
    padded = jnp.pad(padded, ((0, 0), (0, 0), (0, 0), (1, 1)))
    elem_z = three_tap(padded, 3, 1.0 / 6.0, 2.0 / 3.0)
    lapl_z = three_tap(padded, 3, -1.0, 2.0)
    lump_z = three_tap(padded, 3, 1.0 / 3.0, 2.0 / 3.0)
    elem_yz = three_tap(elem_z, 2, 1.0 / 6.0, 2.0 / 3.0)
    lapl_y_elem_z = three_tap(elem_z, 2, -1.0, 2.0)
    elem_y_lapl_z = three_tap(lapl_z, 2, 1.0 / 6.0, 2.0 / 3.0)
    lump_yz = three_tap(lump_z, 2, 1.0 / 3.0, 2.0 / 3.0)
    stiffness = three_tap(elem_yz, 1, -1.0, 2.0) + three_tap(
        lapl_y_elem_z + elem_y_lapl_z, 1, 1.0 / 6.0, 2.0 / 3.0
    )
    mass_sum = three_tap(lump_yz, 1, 1.0 / 3.0, 2.0 / 3.0)
    volume_image = stiffness - medium_term[None] * mass_sum
    flat_image = volume_image.reshape(components, cell_total)
    flat_image = flat_image.at[:, node_cell.reshape(node_total)].add(
        -node_flux.reshape(components, node_total)
    )
    volume_image = flat_image.reshape(components, width_x, width_y, depth_cells)
    slab_rows = boundary_matrix.shape[1]
    column_span = boundary_matrix.shape[2]
    own_rows = slab_rows // col_count
    products = lax.dot_general(
        boundary_matrix.reshape(2 * (own_rows * lax.axis_size("col")), column_span),
        column_traces,
        (((1,), (1,)), ((), ())),
        preferred_element_type=jnp.float32,
    )
    real_part = products[: own_rows * lax.axis_size("col")]
    imag_part = products[own_rows * lax.axis_size("col") :]
    boundary_image = sum_at_owner(
        jnp.concatenate(
            [
                real_part[:, :angles] - imag_part[:, angles:],
                imag_part[:, :angles] + real_part[:, angles:],
            ],
            axis=1,
        ),
        "col",
        0,
    )
    return (volume_image, boundary_image)


def solution(mesh):
    in_specs = (
        P(None, "col", "row", None),
        P("col", "row", None),
        P(None, "col", "row", None),
        P("col", "row", None),
        P("col", "row", None),
        P(None, "row", "col"),
    )
    out_specs = (P(None, "col", "row", None), P(("row", "col"), None))
    return jax.shard_map(
        on_device, mesh=mesh, in_specs=in_specs, out_specs=out_specs, check_vma=False
    )
```

profile of v0, /device:TPU:1, one launch (start us, length us, event | category | flops | bytes accessed | tf_op | source)
XLA Modules:
  0.0 84.1 jit_solution(6091311905287193799)
XLA Ops:
  0.7 2.1 %fusion.19 = (f32[64,4,1,128]{3,2,1,0:T(1,128)S(1)}, f32[64,4,1,128]{3,2,1,0:T(1,128)S(1)}) fusion(f32[64,4,8,128]{3,2,1,0:T(8,128)} %param.6), kind=kLoop, calls=%fused_computation.54 | loop fusion | bytes 524288 | tf_op jit(solution)/shard_map/slice | solution.py:28
  2.8 1.3 %collective-permute-start.1 = (f32[64,4,1,128]{3,0,2,1:T(8,128)S(1)}, f32[64,4,1,128]{3,0,2,1:T(8,128)S(1)}, u32[]{:S(2)}, u32[]{:S(2)}) collective-permute-start(f32[64,4,1,128]{3,0,2,1:T(8,128)S(1)} %copy.46), channel_id=1, source_target_pairs={{32,0},{64,32},{96,64},{128,96},{160,128},{192,160},{224,192},{33,... | collective-permute-start | bytes 393224 | tf_op jit(solution)/shard_map/ppermute | solution.py:30
  4.1 4.7 %collective-permute-start = (f32[64,4,1,128]{3,0,2,1:T(8,128)S(1)}, f32[64,4,1,128]{3,0,2,1:T(8,128)S(1)}, u32[]{:S(2)}, u32[]{:S(2)}) collective-permute-start(f32[64,4,1,128]{3,0,2,1:T(8,128)S(1)} %copy.45), channel_id=1, source_target_pairs={{0,32},{32,64},{64,96},{96,128},{128,160},{160,192},{192,224},{1,3... | collective-permute-start | bytes 393224 | tf_op jit(solution)/shard_map/ppermute | solution.py:27
  8.9 1.8 %copy.38 = bf16[64,4,8,128]{0,3,2,1:T(8,128)(2,1)S(1)} copy(f32[64,4,8,128]{3,2,1,0:T(8,128)} %param.6) | data formatting | bytes 1572864 | tf_op args[0]
  10.9 0.3 select_reduce_fusion
  11.4 1.4 %gather_fusion = bf16[384,64]{1,0:T(8,128)(2,1)S(1)} fusion(bf16[64,4096]{0,1:T(8,128)(2,1)S(1)} %bitcast.32, s32[1024]{0:T(1024)S(1)} %pad_clamp_fusion), kind=kCustom, calls=%fused_computation | custom fusion | bytes 99840 | tf_op jit(solution)/shard_map/jit(_take)/gather | solution.py:70
  13.2 0.1 copy.32
  13.3 0.2 pad_maximum_fusion.3
  13.5 5.1 %collective-permute-start.3 = (f32[64,1,10,128]{3,2,1,0:T(8,128)S(1)}, f32[64,1,10,128]{3,2,1,0:T(8,128)S(1)}, u32[]{:S(2)}, u32[]{:S(2)}) collective-permute-start(f32[64,1,10,128]{3,2,1,0:T(8,128)S(1)} %get-tuple-element.16), channel_id=1, source_target_pairs={{1,0},{2,1},{3,2},{4,3},{5,4},{6,5},{7,6},{8,7},{9,8},{10,9},{11,1... | collective-permute-start | bytes 983048 | tf_op jit(solution)/shard_map/ppermute | solution.py:30
  18.6 1.9 %collective-permute-start.2 = (f32[64,1,10,128]{3,2,1,0:T(8,128)S(1)}, f32[64,1,10,128]{3,2,1,0:T(8,128)}, u32[]{:S(2)}, u32[]{:S(2)}) collective-permute-start(f32[64,1,10,128]{3,2,1,0:T(8,128)S(1)} %get-tuple-element.15), channel_id=1, source_target_pairs={{0,1},{1,2},{2,3},{3,4},{4,5},{5,6},{6,7},{7,8},{8,9},{9,10},{10,1... | collective-permute-start | bytes 983048 | tf_op jit(solution)/shard_map/ppermute | solution.py:27
  20.7 0.8 reshape.153
  21.5 13.0 %all-to-all-start = ((bf16[32,2,384]{2,1,0:T(2,128)(2,1)}), bf16[32,2,384]{2,1,0:T(2,128)(2,1)S(1)}, u32[]{:S(2)}, u32[]{:S(2)}) async-start(bf16[32,2,384]{2,1,0:T(2,128)(2,1)} %reshape.153), calls=%async_computation | async-start | bytes 98304 | tf_op jit(solution)/shard_map/all_to_all | solution.py:71
  34.6 0.8 copy.47
  35.4 0.6 fusion.17
  36.0 8.6 %all-to-all-done = bf16[32,2,384]{2,1,0:T(2,128)(2,1)S(1)} async-done(((bf16[32,2,384]{2,1,0:T(2,128)(2,1)}), bf16[32,2,384]{2,1,0:T(2,128)(2,1)S(1)}, u32[]{:S(2)}, u32[]{:S(2)}) %all-to-all-start) | async-done | bytes 49184 | tf_op jit(solution)/shard_map/all_to_all | solution.py:71
  44.9 0.8 broadcast_in_dim.51
  45.7 5.5 %all-to-all-start.1 = ((bf16[8,64,384]{2,1,0:T(8,128)(2,1)}), bf16[8,64,384]{2,1,0:T(8,128)(2,1)S(1)}, u32[]{:S(2)}, u32[]{:S(2)}) async-start(bf16[8,64,384]{2,1,0:T(8,128)(2,1)} %broadcast_in_dim.51), calls=%async_computation.1 | async-start | bytes 786432 | tf_op jit(solution)/shard_map/all_to_all | solution.py:15
  51.2 1.5 %pad_maximum_fusion = f32[64,6,10,128]{3,2,1,0:T(8,128)S(1)} fusion(f32[64,1,10,128]{3,2,1,0:T(8,128)S(1)} %collective-permute-done.3, f32[64,4,1,128]{3,2,1,0:T(1,128)S(1)} %copy.33, f32[64,4,8,128]{3,2,1,0:T(8,128)S(1)} %copy-done, f32[64,4,1,128]{3,2,1,0:T(1,128)S(1)} %copy.32, f32[64,1,10,128]{3,2,1,0:T(8,128)} %collective-permute-done.2), kind=kLoop, calls=%fused_computation.5 | loop fusion | flops 1966080 | bytes 3932160 | tf_op jit(solution)/shard_map/concatenate | solution.py:31
  52.7 5.0 %multiply_add_fusion.2 = (f32[64,6,10,128]{3,2,1,0:T(8,128)S(1)}, f32[64,6,10,128]{3,2,1,0:T(8,128)S(1)}, f32[64,6,10,128]{3,2,1,0:T(8,128)S(1)}) fusion(f32[64,6,10,128]{3,2,1,0:T(8,128)S(1)} %pad_maximum_fusion), kind=kLoop, calls=%fused_computation.8 | loop fusion | flops 5406720 | bytes 7864320 | tf_op jit(solution)/shard_map/add | solution.py:52
  57.7 1.6 %fusion.1 = f32[64,6,8,128]{3,2,1,0:T(8,128)} fusion(f32[64,6,10,128]{3,2,1,0:T(8,128)S(1)} %get-tuple-element.14), kind=kLoop, calls=%fused_computation.10 | loop fusion | flops 1572864 | bytes 6291456 | tf_op jit(solution)/shard_map/add | solution.py:52
  59.3 1.0 %multiply_add_fusion.3 = (f32[64,6,8,128]{3,2,1,0:T(8,128)S(1)}, f32[64,6,8,128]{3,2,1,0:T(8,128)S(1)}) fusion(f32[64,6,10,128]{3,2,1,0:T(8,128)S(1)} %get-tuple-element.12, f32[64,6,10,128]{3,2,1,0:T(8,128)S(1)} %get-tuple-element.13), kind=kLoop, calls=%fused_computation.19 | loop fusion | flops 4718592 | bytes 12582912 | tf_op jit(solution)/shard_map/add | solution.py:52
  60.4 4.8 %convolution_bitcast_fusion = f32[1024,64]{0,1:T(8,128)S(1)} fusion(bf16[64,3072]{1,0:T(8,128)(2,1)S(1)} %bitcast.34, bf16[1024,3072]{1,0:T(8,128)(2,1)} %bitcast.31), kind=kOutput, calls=%fused_computation.20 | convolution fusion | flops 402653184 | bytes 6946816 | tf_op jit(solution)/shard_map/dot_general | solution.py:95
  65.4 0.8 reshape.155
  66.2 4.2 %all-to-all-start.2 = ((f32[32,1,1024]{2,1,0:T(1,128)}), f32[32,1,1024]{2,1,0:T(1,128)S(1)}, u32[]{:S(2)}, u32[]{:S(2)}) async-start(f32[32,1,1024]{2,1,0:T(1,128)} %reshape.155), calls=%async_computation.2 | async-start | bytes 262144 | tf_op jit(solution)/shard_map/all_to_all | solution.py:43
  70.4 3.5 %fusion.8 = f32[64,4,8,128]{3,2,1,0:T(8,128)} fusion(f32[64,6,8,128]{3,2,1,0:T(8,128)} %fusion.1, f32[64,6,8,128]{3,2,1,0:T(8,128)S(1)} %get-tuple-element.11, f32[64,6,8,128]{3,2,1,0:T(8,128)S(1)} %get-tuple-element.10, f32[4,8,128]{2,1,0:T(8,128)S(1)} %copy-done.3), kind=kLoop, calls=%fused_computation.24 | loop fusion | flops 3932160 | bytes 10502144 | tf_op jit(solution)/shard_map/sub | solution.py:86
  73.9 1.9 %copy.34 = f32[64,4,8,128]{0,3,2,1:T(8,128)S(1)} copy(f32[64,4,8,128]{3,2,1,0:T(8,128)} %fusion.8) | data formatting | bytes 2097152 | tf_op jit(solution)/shard_map/sub | solution.py:86
  75.8 3.7 %scatter_custom_fusion = f32[64,4096]{0,1:T(8,128)S(1)} fusion(f32[64,4096]{0,1:T(8,128)S(1)} %bitcast.29, s32[384]{0:T(512)} %fusion.17, f32[64,1,1,384]{0,3,1,2:T(8,128)S(1)} %copy-done.1), kind=kCustom, calls=%fused_computation.40 | custom fusion | flops 24576 | bytes 1245184 | tf_op jit(solution)/shard_map/scatter-add | solution.py:88
  79.5 1.8 %copy.43 = f32[64,4,8,128]{3,2,1,0:T(8,128)} copy(f32[64,4,8,128]{0,3,2,1:T(8,128)S(1)} %bitcast.30) | data formatting | bytes 2097152
  81.3 0.6 all-to-all-done.2
  81.9 0.5 broadcast.88
  82.4 0.9 %reduce.5 = f32[32,1024]{1,0:T(8,128)S(1)} reduce(f32[32,1,1024]{2,1,0:T(1,128)S(1)} %all-to-all-done.2, f32[]{:T(128)} %broadcast.88), dimensions={1}, to_apply=%all_to_all.12.reduce_sub_computation | reduce | bytes 262148 | tf_op jit(solution)/shard_map/all_to_all | solution.py:43
  83.5 0.6 reduce_sum.19
  (41 shorter events, 1.6 us)
Async XLA Ops:
  0.6 12.7 %copy-start = (f32[64,4,8,128]{3,2,1,0:T(8,128)S(1)}, f32[64,4,8,128]{3,2,1,0:T(8,128)}, u32[]{:S(2)}) copy-start(f32[64,4,8,128]{3,2,1,0:T(8,128)} %param.6) | copy-start | bytes 3145732
  0.6 10.0 %copy-start.4 = (s32[1,1,384]{2,1,0:T(1,128)S(1)}, s32[1,1,384]{2,1,0:T(1,128)}, u32[]{:S(2)}) copy-start(s32[1,1,384]{2,1,0:T(1,128)} %param.9) | copy-start | bytes 4612
  0.7 10.2 %copy-start.5 = (s32[1,1,32]{2,1,0:T(1,128)S(1)}, s32[1,1,32]{2,1,0:T(1,128)}, u32[]{:S(2)}) copy-start(s32[1,1,32]{2,1,0:T(1,128)} %param.10) | copy-start | bytes 388
  2.8 10.2 %collective-permute-start.1 = (f32[64,4,1,128]{3,0,2,1:T(8,128)S(1)}, f32[64,4,1,128]{3,0,2,1:T(8,128)S(1)}, u32[]{:S(2)}, u32[]{:S(2)}) collective-permute-start(f32[64,4,1,128]{3,0,2,1:T(8,128)S(1)} %copy.46), channel_id=1, source_target_pairs={{32,0},{64,32},{96,64},{128,96},{160,128},{192,160},{224,192},{33,... | collective-permute-start | bytes 393224 | tf_op jit(solution)/shard_map/ppermute | solution.py:30
  4.1 30.3 %copy-start.2 = (f32[64,1,1,384]{3,2,1,0:T(1,128)S(1)}, f32[64,1,1,384]{3,2,1,0:T(1,128)}, u32[]{:S(2)}) copy-start(f32[64,1,1,384]{3,2,1,0:T(1,128)} %param.8) | copy-start | bytes 294916
  4.1 9.0 %collective-permute-start = (f32[64,4,1,128]{3,0,2,1:T(8,128)S(1)}, f32[64,4,1,128]{3,0,2,1:T(8,128)S(1)}, u32[]{:S(2)}, u32[]{:S(2)}) collective-permute-start(f32[64,4,1,128]{3,0,2,1:T(8,128)S(1)} %copy.45), channel_id=1, source_target_pairs={{0,32},{32,64},{64,96},{96,128},{128,160},{160,192},{192,224},{1,3... | collective-permute-start | bytes 393224 | tf_op jit(solution)/shard_map/ppermute | solution.py:27
  13.5 37.6 %collective-permute-start.3 = (f32[64,1,10,128]{3,2,1,0:T(8,128)S(1)}, f32[64,1,10,128]{3,2,1,0:T(8,128)S(1)}, u32[]{:S(2)}, u32[]{:S(2)}) collective-permute-start(f32[64,1,10,128]{3,2,1,0:T(8,128)S(1)} %get-tuple-element.16), channel_id=1, source_target_pairs={{1,0},{2,1},{3,2},{4,3},{5,4},{6,5},{7,6},{8,7},{9,8},{10,9},{11,1... | collective-permute-start | bytes 983048 | tf_op jit(solution)/shard_map/ppermute | solution.py:30
  18.6 32.5 %collective-permute-start.2 = (f32[64,1,10,128]{3,2,1,0:T(8,128)S(1)}, f32[64,1,10,128]{3,2,1,0:T(8,128)}, u32[]{:S(2)}, u32[]{:S(2)}) collective-permute-start(f32[64,1,10,128]{3,2,1,0:T(8,128)S(1)} %get-tuple-element.15), channel_id=1, source_target_pairs={{0,1},{1,2},{2,3},{3,4},{4,5},{5,6},{6,7},{7,8},{8,9},{9,10},{10,1... | collective-permute-start | bytes 983048 | tf_op jit(solution)/shard_map/ppermute | solution.py:27
  21.5 23.2 %all-to-all-start = ((bf16[32,2,384]{2,1,0:T(2,128)(2,1)}), bf16[32,2,384]{2,1,0:T(2,128)(2,1)S(1)}, u32[]{:S(2)}, u32[]{:S(2)}) async-start(bf16[32,2,384]{2,1,0:T(2,128)(2,1)} %reshape.153), calls=%async_computation | async-start | bytes 98304 | tf_op jit(solution)/shard_map/all_to_all | solution.py:71
  45.7 14.6 %all-to-all-start.1 = ((bf16[8,64,384]{2,1,0:T(8,128)(2,1)}), bf16[8,64,384]{2,1,0:T(8,128)(2,1)S(1)}, u32[]{:S(2)}, u32[]{:S(2)}) async-start(bf16[8,64,384]{2,1,0:T(8,128)(2,1)} %broadcast_in_dim.51), calls=%async_computation.1 | async-start | bytes 786432 | tf_op jit(solution)/shard_map/all_to_all | solution.py:15
  60.4 10.0 %copy-start.3 = (f32[4,8,128]{2,1,0:T(8,128)S(1)}, f32[4,8,128]{2,1,0:T(8,128)}, u32[]{:S(2)}) copy-start(f32[4,8,128]{2,1,0:T(8,128)} %param.7) | copy-start | bytes 49156
  66.2 15.7 %all-to-all-start.2 = ((f32[32,1,1024]{2,1,0:T(1,128)}), f32[32,1,1024]{2,1,0:T(1,128)S(1)}, u32[]{:S(2)}, u32[]{:S(2)}) async-start(f32[32,1,1024]{2,1,0:T(1,128)} %reshape.155), calls=%async_computation.2 | async-start | bytes 262144 | tf_op jit(solution)/shard_map/all_to_all | solution.py:43
  73.9 1.9 %copy-start.1 = (f32[64,1,1,384]{0,3,1,2:T(8,128)S(1)}, f32[64,1,1,384]{0,3,1,2:T(8,128)}, u32[]{:S(2)}) copy-start(f32[64,1,1,384]{0,3,1,2:T(8,128)} %copy.47) | copy-start | bytes 294916
where the time goes:
time: 84.7 us; the launch traced here: 84.1 us
  starting transfers between devices  35.6 us (42%)
  other arithmetic  19.3 us (23%)
  local copies, waits for them, and re-layouts  14.1 us (17%)
  waiting for transfers between devices  9.24 us (11%)
  matrix products  4.81 us (6%)
  between operations  0.99 us (1%)
    all_to_all x1, starting transfers between devices, on_device(): lax.all_to_all(traces, 'col', split_axis=1, concat_axis=1, tiled=True)  13 us
    all_to_all x1, waiting for transfers between devices, on_device(): lax.all_to_all(traces, 'col', split_axis=1, concat_axis=1, tiled=True)  8.63 us
    add x3, other arithmetic, three_tap(): return side_weight * (lower + upper) + centre_weight * middle  7.61 us
    ppermute x2, starting transfers between devices, padded_2(): lax.ppermute(lax.slice_in_dim(block, block.shape[dim] - width, None, axis...  6.62 us
    ppermute x2, starting transfers between devices, padded_2(): lax.ppermute(lax.slice_in_dim(block, 0, width, axis=dim), axis, backward)  6.39 us
    all_to_all x1, starting transfers between devices, sent_to_all(): lax.all_to_all(jnp.broadcast_to(x[None], (count, *x.shape)), axis, 0, 0,...  5.45 us
    unnamed x20, local copies, waits for them, and re-layouts  5.44 us
    dot_general x1, matrix products, on_device(): lax.dot_general(boundary_matrix.reshape(2 * (own_rows * lax.axis_size('co...  4.81 us
  transfers between devices with their start and end apart: 7, of which 2 were waited for; matrix products, arithmetic and copies ran while one was open for 33% of the time, Pallas kernels for 0%

commit v1 on v0

v1 whole, which is shorter than its diff:
```python
import functools

import jax
import jax.numpy as jnp
from jax import lax
from jax.experimental import pallas as pl
from jax.experimental.pallas import tpu as pltpu
from jax.sharding import PartitionSpec as P

MESH = pl.DeviceIdType.MESH
F32 = jnp.float32
BF16 = jnp.bfloat16
GROUPS = 4


def iota(shape, dim):
    return lax.broadcasted_iota(jnp.int32, shape, dim)


def nt_dot(a, b):
    return lax.dot_general(a, b, (((1,), (1,)), ((), ())), preferred_element_type=F32)


def nn_dot(a, b):
    return lax.dot_general(a, b, (((1,), (0,)), ((), ())), preferred_element_type=F32)


def row_at(me_r, step, rows):
    wide = rows // 2
    if wide == 4:
        third = step % 3
        near = step < 6
        dz = jnp.where(near, step // 3, step - 6)
        dx = jnp.where(near, third + third // 2, 2)
    else:
        dz, dx = step // wide, step % wide
    z = (me_r // wide + dz) % 2
    x = (me_r % wide + dx) % wide
    return z * wide + x


def kernel(
    rows, cols,
    wave_in, medium_in, flux_in, cell_in, target_in, matrix_in,
    volume_out, boundary_out,
    wave, medium, flux, cell, target, matrix, onehot, picked, slots, traces, total, parts, landed,
    volume, faces, edges, corners, faces_in, edges_in, corners_in, faces_f, edges_f, corners_f,
    in_sem, out_sem, slot_send, slot_recv, row_send, row_recv, part_send, part_recv, halo_send, halo_recv,
):
    me_r = lax.axis_index("row")
    me_c = lax.axis_index("col")
    comps = wave.shape[0] // 32
    nodes = cell.shape[1]
    slot_len = nodes // cols
    half_slot = slot_len // 2
    span = cols // GROUPS
    my_group = me_c // span

    loads = [
        pltpu.make_async_copy(src, dst, in_sem.at[i])
        for i, (src, dst) in enumerate(
            [
                (cell_in, cell),
                (target_in, target),
                (wave_in, wave),
                (flux_in, flux),
                (medium_in, medium),
                (matrix_in, matrix),
            ]
        )
    ]
    for load in loads:
        load.start()

    barrier = pltpu.get_barrier_semaphore()

    def greet(r, c):
        pl.semaphore_signal(barrier, inc=1, device_id=(r, c), device_id_type=MESH)

    @pl.loop(1, cols)
    def _(i):
        greet(me_r, (me_c + i) % cols)

    @pl.loop(1, rows)
    def _(i):
        greet((me_r + i) % rows, me_c)

    partners = [(0, -1), (0, 1), (-1, 0), (1, 0), (-1, -1), (1, -1), (-1, 1), (1, 1)]

    def inside(step):
        dr, dc = step
        ok = None
        for d, me, n in ((dr, me_r, rows), (dc, me_c, cols)):
            if d:
                one = me + d >= 0 if d < 0 else me + d < n
                ok = one if ok is None else jnp.logical_and(ok, one)
        return ok

    for step in partners[4:]:

        @pl.when(inside(step))
        def _():
            greet(me_r + step[0], me_c + step[1])

    loads[0].wait()
    loads[1].wait()
    cells = cell[...]
    place = cells // 128
    onehot[...] = jnp.where(iota((128, nodes), 0) == cells % 128, 1.0, 0.0).astype(BF16)
    node = iota((1, nodes), 1)
    spread = jnp.where(iota((cols, nodes), 0) == iota((cols, nodes), 1) // slot_len, 1.0, 0.0)
    wanted = jnp.broadcast_to(target[...].astype(F32), (8, cols))
    wanted = nn_dot(wanted.astype(BF16), spread.astype(BF16))[:1].astype(jnp.int32)
    within = node % slot_len
    row_of = wanted * 8 + within % half_slot
    lane_half = within // half_slot

    loads[2].wait()
    here = iota((32, nodes), 0) == place

    @pl.loop(0, comps // 8)
    def _(i):
        start = pl.multiple_of(i * 256, 256)
        found = nn_dot(wave[pl.ds(start, 256), :].astype(BF16), onehot[...])
        found = jnp.where(here[None], found.reshape(8, 32, nodes), 0.0)
        found = found.reshape(8, 4, 8, nodes)
        found = (found[:, 0] + found[:, 1]) + (found[:, 2] + found[:, 3])
        picked[pl.ds(pl.multiple_of(i * 64, 64), 64), :] = found.reshape(64, nodes).astype(BF16)

    gather = jnp.where(iota((comps, comps * 8), 0) == iota((comps, comps * 8), 1) // 8, 1.0, 0.0)
    trace = nn_dot(gather.astype(BF16), picked[...])
    blank = jnp.zeros_like(trace)
    sent = None
    for half in range(2):
        match = jnp.logical_and(iota((cols * 8, nodes), 0) == row_of, lane_half == half)
        order = jnp.where(match, 1.0, 0.0).astype(BF16)
        pair = [trace, blank] if half == 0 else [blank, trace]
        term = nt_dot(order, jnp.concatenate(pair, axis=0).astype(BF16))
        sent = term if sent is None else sent + term
    slots[...] = sent.reshape(cols, 8, 2 * comps).astype(BF16)

    beside_r = jnp.where(me_r > 0, 1, 0) + jnp.where(me_r < rows - 1, 1, 0)
    beside_c = jnp.where(me_c > 0, 1, 0) + jnp.where(me_c < cols - 1, 1, 0)
    pl.semaphore_wait(barrier, cols - 1 + rows - 1 + beside_r * beside_c)

    def slot_copy(t):
        return pltpu.make_async_remote_copy(
            src_ref=slots.at[t],
            dst_ref=traces.at[me_r, me_c],
            send_sem=slot_send.at[t],
            recv_sem=slot_recv.at[me_c],
            device_id=(me_r, t),
            device_id_type=MESH,
        )

    def slot_arrival(c):
        return pltpu.make_async_remote_copy(
            src_ref=slots.at[c],
            dst_ref=traces.at[me_r, c],
            send_sem=slot_send.at[c],
            recv_sem=slot_recv.at[c],
            device_id=(me_r, c),
            device_id_type=MESH,
        )

    own_slot = pltpu.make_async_copy(slots.at[me_c], traces.at[me_r, me_c], slot_recv.at[me_c])
    for hop in (2, 1, 3, 0):
        first = ((my_group + hop) % GROUPS) * span

        @pl.loop(0, span)
        def _(i):
            t = first + i

            @pl.when(t != me_c)
            def _():
                slot_copy(t).start()

    own_slot.start()

    for side in range(2):

        @pl.loop(0, comps // 8)
        def _(i):
            rows_of = [wave[pl.ds(i * 256 + j * 32 + side * 24, 8), :] for j in range(8)]
            outer = jnp.concatenate(rows_of, axis=0).astype(BF16)
            faces[side, pl.ds(pl.multiple_of(i * 64, 64), 64), :] = outer

    for side in range(2):
        lane_y = 0 if side == 0 else 7
        edges[side] = wave[pl.ds(lane_y, comps * 4, stride=8), :].astype(BF16)
        corners[side] = wave[pl.ds(lane_y, comps, stride=32), :].astype(BF16)
        corners[2 + side] = wave[pl.ds(24 + lane_y, comps, stride=32), :].astype(BF16)

    halo_parts = [
        (faces.at[0], faces_in.at[1]),
        (faces.at[1], faces_in.at[0]),
        (edges.at[0], edges_in.at[1]),
        (edges.at[1], edges_in.at[0]),
        (corners.at[0], corners_in.at[3]),
        (corners.at[1], corners_in.at[2]),
        (corners.at[2], corners_in.at[1]),
        (corners.at[3], corners_in.at[0]),
    ]
    opposite = [1, 0, 3, 2, 7, 6, 5, 4]

    def halo_copy(k):
        return pltpu.make_async_remote_copy(
            src_ref=halo_parts[k][0],
            dst_ref=halo_parts[k][1],
            send_sem=halo_send.at[k],
            recv_sem=halo_recv.at[k],
            device_id=(me_r + partners[k][0], me_c + partners[k][1]),
            device_id_type=MESH,
        )

    for k in range(8):

        @pl.when(inside(partners[k]))
        def _():
            halo_copy(k).start()

    loads[3].wait()

    @pl.loop(0, comps // 8)
    def _(i):
        start = pl.multiple_of(i * 256, 256)
        wide = jnp.where(here[None], flux[pl.ds(i * 8, 8), :, :], 0.0).reshape(256, nodes)
        upper = wide.astype(BF16)
        lower = (wide - upper.astype(F32)).astype(BF16)
        volume[pl.ds(start, 256), :] = nt_dot(upper, onehot[...]) + nt_dot(lower, onehot[...])

    def row_copy(r, g):
        block = traces.at[me_r, pl.ds(g * span, span)]
        return pltpu.make_async_remote_copy(
            src_ref=block,
            dst_ref=block,
            send_sem=row_send.at[r, g],
            recv_sem=row_recv.at[me_r, g],
            device_id=(r, me_c),
            device_id_type=MESH,
        )

    def row_arrival(r, g):
        block = traces.at[r, pl.ds(g * span, span)]
        return pltpu.make_async_remote_copy(
            src_ref=block,
            dst_ref=block,
            send_sem=row_send.at[r, g],
            recv_sem=row_recv.at[r, g],
            device_id=(r, me_c),
            device_id_type=MESH,
        )

    for hop in (0, 1, 3, 2):
        g = (my_group + hop) % GROUPS

        @pl.loop(0, span)
        def _(i):
            slot_arrival(g * span + i).wait_recv()

        @pl.loop(1, rows)
        def _(i):
            row_copy(row_at(me_r, rows - i, rows), g).start()

    loads[5].wait()
    total[...] = jnp.zeros_like(total)
    left = iota((cols * 8, 128), 1) < comps
    minus = iota((cols * 8, 128), 1) % comps < comps // 2
    to_node = iota((nodes, cols * 8), 0)
    packed = iota((nodes, cols * 8), 1)
    unpack = []
    for half in range(2):
        hit = jnp.logical_and(
            to_node == (packed // 8) * slot_len + packed % 8 + half * half_slot,
            packed % 8 < half_slot,
        )
        unpack.append(jnp.where(hit, 1.0, 0.0).astype(BF16))
    unpack = jnp.concatenate(unpack, axis=1)

    @pl.loop(0, rows)
    def _(step):
        r = row_at(me_r, step, rows)

        @pl.when(step > 0)
        def _():
            @pl.loop(0, GROUPS)
            def _(g):
                row_arrival(r, g).wait_recv()

        raw = traces[r].reshape(cols * 8, 2 * comps).astype(F32)
        turned = pltpu.roll(raw, comps, 1)
        stacked = []
        for half in range(2):
            same = jnp.where(left, raw, turned) if half == 0 else jnp.where(left, turned, raw)
            swapped = pltpu.roll(same, comps // 2, 1)
            swapped = jnp.where(minus, -swapped, swapped)
            stacked.append(jnp.concatenate([same, swapped], axis=1).astype(BF16))
        both = nn_dot(unpack, jnp.concatenate(stacked, axis=0)).astype(BF16)
        columns = pl.ds(pl.multiple_of(r * nodes, nodes), nodes)
        total[...] += nn_dot(matrix[0, :, columns], both[:, :128]) + nn_dot(
            matrix[1, :, columns], both[:, 128:]
        )

    tiles = total[...].reshape(cols, 2, 8, 128)
    parts[...] = jnp.where(
        iota((cols, 8, 128), 2) < comps, tiles[:, 0], tiles[:, 1]
    ).astype(BF16)

    def part_copy(t):
        return pltpu.make_async_remote_copy(
            src_ref=parts.at[t],
            dst_ref=landed.at[me_c],
            send_sem=part_send.at[t],
            recv_sem=part_recv.at[me_c],
            device_id=(me_r, t),
            device_id_type=MESH,
        )

    def part_arrival(c):
        return pltpu.make_async_remote_copy(
            src_ref=parts.at[c],
            dst_ref=landed.at[c],
            send_sem=part_send.at[c],
            recv_sem=part_recv.at[c],
            device_id=(me_r, c),
            device_id_type=MESH,
        )

    own_part = pltpu.make_async_copy(parts.at[me_c], landed.at[me_c], part_recv.at[me_c])
    for hop in (2, 1, 3, 0):
        first = ((my_group + hop) % GROUPS) * span

        @pl.loop(0, span)
        def _(i):
            t = first + i

            @pl.when(t != me_c)
            def _():
                part_copy(t).start()

    own_part.start()

    spread_to = [faces_f.at[0], faces_f.at[1], edges_f.at[0], edges_f.at[1]] + [
        corners_f.at[k] for k in range(4)
    ]
    come_from = [faces_in.at[0], faces_in.at[1], edges_in.at[0], edges_in.at[1]] + [
        corners_in.at[k] for k in range(4)
    ]
    for k in range(8):

        @pl.when(inside(partners[k]))
        def _():
            halo = pltpu.make_async_remote_copy(
                src_ref=come_from[k],
                dst_ref=come_from[k],
                send_sem=halo_send.at[k],
                recv_sem=halo_recv.at[opposite[k]],
                device_id=(me_r + partners[k][0], me_c + partners[k][1]),
                device_id_type=MESH,
            )
            halo.wait_recv()
            spread_to[k][...] = come_from[k][...].astype(F32)

        @pl.when(jnp.logical_not(inside(partners[k])))
        def _():
            spread_to[k][...] = jnp.zeros(spread_to[k].shape, F32)

    loads[4].wait()
    sublane = iota((8, 128), 0)
    lane = iota((8, 128), 1)

    def depth_sides(v):
        below = jnp.where(lane == 0, 0.0, pltpu.roll(v, 1, 1))
        above = jnp.where(lane == 127, 0.0, pltpu.roll(v, 127, 1))
        return below + above

    def layer(u, low, high):
        below = jnp.where(sublane == 0, jnp.broadcast_to(low, (8, 128)), pltpu.roll(u, 1, 0))
        above = jnp.where(sublane == 7, jnp.broadcast_to(high, (8, 128)), pltpu.roll(u, 7, 0))
        sides = below + above
        outer = depth_sides(sides)
        ring = 2.0 * (sides + depth_sides(u)) + outer
        return u, outer, ring, 4.0 * u + ring

    @pl.loop(0, comps)
    def _(k):
        layers = []
        for x in range(6):
            if x in (0, 5):
                side = 0 if x == 0 else 1
                u = faces_f[side, pl.ds(pl.multiple_of(k * 8, 8), 8), :]
                low = corners_f[2 * side, pl.ds(k, 1), :]
                high = corners_f[2 * side + 1, pl.ds(k, 1), :]
            else:
                u = wave[pl.ds(pl.multiple_of(k * 32 + (x - 1) * 8, 8), 8), :]
                low = edges_f[0, pl.ds(k * 4 + x - 1, 1), :]
                high = edges_f[1, pl.ds(k * 4 + x - 1, 1), :]
            layers.append(layer(u, low, high))
        for x in range(1, 5):
            u, outer, ring, mass = layers[x]
            stiffness = (8.0 / 3.0) * u - (1.0 / 6.0) * outer
            stiffness -= (1.0 / 12.0) * (layers[x - 1][2] + layers[x + 1][2])
            mass_sum = (2.0 * mass + (layers[x - 1][3] + layers[x + 1][3])) * (1.0 / 27.0)
            where = pl.ds(pl.multiple_of(k * 32 + (x - 1) * 8, 8), 8)
            volume[where, :] = (
                stiffness - medium[pl.ds((x - 1) * 8, 8), :] * mass_sum - volume[where, :]
            )

    store = pltpu.make_async_copy(volume, volume_out, out_sem)
    store.start()

    @pl.loop(0, cols)
    def _(c):
        part_arrival(c).wait_recv()

    sums = jnp.sum(landed[...].astype(F32), axis=0)
    boundary_out[0:8, :] = sums[:, :comps]
    boundary_out[8:16, :] = pltpu.roll(sums, comps, 1)[:, :comps]

    @pl.loop(0, cols)
    def _(t):
        @pl.when(t != me_c)
        def _():
            slot_copy(t).wait_send()
            part_copy(t).wait_send()

    @pl.loop(1, rows)
    def _(i):
        @pl.loop(0, GROUPS)
        def _(g):
            row_copy((me_r + i) % rows, g).wait_send()

    for k in range(8):

        @pl.when(inside(partners[k]))
        def _():
            halo_copy(k).wait_send()

    store.wait()


def on_device(rows, cols, wave_field, medium_term, node_flux, node_cell, block_target, boundary_matrix):
    comps = wave_field.shape[0]
    nodes = node_cell.shape[-1]
    slab_rows, width = boundary_matrix.shape[1:]
    own_rows = slab_rows // cols
    vmem = pltpu.VMEM
    dma = pltpu.SemaphoreType.DMA
    volume, boundary = pl.pallas_call(
        functools.partial(kernel, rows, cols),
        out_shape=(
            jax.ShapeDtypeStruct((comps * 32, 128), F32),
            jax.ShapeDtypeStruct((own_rows, comps), F32),
        ),
        in_specs=[pl.BlockSpec(memory_space=pltpu.HBM)] * 6,
        out_specs=(pl.BlockSpec(memory_space=pltpu.HBM), pl.BlockSpec(memory_space=pltpu.VMEM)),
        scratch_shapes=[
            vmem((comps * 32, 128), F32),
            vmem((32, 128), F32),
            vmem((comps, 1, nodes), F32),
            vmem((1, nodes), jnp.int32),
            vmem((1, cols), jnp.int32),
            vmem((2, slab_rows, width), BF16),
            vmem((128, nodes), BF16),
            vmem((comps * 8, nodes), BF16),
            vmem((cols, 8, 128), BF16),
            vmem((rows, cols, 8, 128), BF16),
            vmem((slab_rows, 128), F32),
            vmem((cols, 8, 128), BF16),
            vmem((cols, 8, 128), BF16),
            vmem((comps * 32, 128), F32),
            vmem((2, comps * 8, 128), BF16),
            vmem((2, comps * 4, 128), BF16),
            vmem((4, comps, 128), BF16),
            vmem((2, comps * 8, 128), BF16),
            vmem((2, comps * 4, 128), BF16),
            vmem((4, comps, 128), BF16),
            vmem((2, comps * 8, 128), F32),
            vmem((2, comps * 4, 128), F32),
            vmem((4, comps, 128), F32),
            dma((6,)),
            dma(()),
            dma((cols,)),
            dma((cols,)),
            dma((rows, GROUPS)),
            dma((rows, GROUPS)),
            dma((cols,)),
            dma((cols,)),
            dma((8,)),
            dma((8,)),
        ],
        compiler_params=pltpu.CompilerParams(
            collective_id=0, has_side_effects=True, vmem_limit_bytes=63_000_000
        ),
        name="coupled_apply",
    )(
        wave_field.reshape(comps * 32, 128),
        medium_term.reshape(32, 128),
        node_flux.reshape(comps, 1, nodes),
        node_cell.reshape(1, nodes),
        block_target.reshape(1, cols),
        boundary_matrix,
    )
    return volume.reshape(wave_field.shape), boundary


def solution(mesh):
    in_specs = (
        P(None, "col", "row", None),
        P("col", "row", None),
        P(None, "col", "row", None),
        P("col", "row", None),
        P("col", "row", None),
        P(None, "row", "col"),
    )
    out_specs = (P(None, "col", "row", None), P(("row", "col"), None))
    return jax.shard_map(
        functools.partial(on_device, mesh.shape["row"], mesh.shape["col"]),
        mesh=mesh,
        in_specs=in_specs,
        out_specs=out_specs,
        check_vma=False,
    )
```

time: 84.7 us -> 43.7 us (0.52)
  Pallas kernels: 0 us -> 39.2 us
  starting transfers between devices: 35.6 us -> 0 us
  other arithmetic: 19.3 us -> 0 us
  local copies, waits for them, and re-layouts: 14.1 us -> 3.56 us
  waiting for transfers between devices: 9.24 us -> 0 us
  matrix products: 4.81 us -> 0 us
    pallas_call x0 -> x1, Pallas kernels: none -> 39.2 us  [on_device(): pl.pallas_call(functools.partial(kernel, rows, cols), out_shape=(jax.Shap...]
    all_to_all x3 -> x0, starting transfers between devices: 22.6 us -> none  [the longest x1 13 us: on_device(): lax.all_to_all(traces, 'col', split_axis=1, concat_axis=1, tiled=True)]
    ppermute x4 -> x0, starting transfers between devices: 13 us -> none  [the longest x2 6.62 us: padded_2(): lax.ppermute(lax.slice_in_dim(block, block.shape[dim] - width, None, axis...]
    all_to_all x3 -> x0, waiting for transfers between devices: 9.23 us -> none  [the longest x1 8.63 us: on_device(): lax.all_to_all(traces, 'col', split_axis=1, concat_axis=1, tiled=True)]
    add x3 -> x0, other arithmetic: 7.61 us -> none  [three_tap(): return side_weight * (lower + upper) + centre_weight * middle]
    dot_general x1 -> x0, matrix products: 4.81 us -> none  [on_device(): lax.dot_general(boundary_matrix.reshape(2 * (own_rows * lax.axis_size('co...]
    scatter-add x1 -> x0, other arithmetic: 3.7 us -> none  [on_device(): flat_image.at[:, node_cell.reshape(node_total)]]
    sub x2 -> x0, other arithmetic: 3.54 us -> none  [the longest x1 3.52 us: on_device(): volume_image = stiffness - medium_term[None] * mass_sum]
  transfers between devices with their start and end apart: 7 -> 0, of which waited for: 2 -> 0; matrix products, arithmetic and copies ran while one was open for 33% -> 0% of each run, Pallas kernels for 0% -> 0%
where the time goes in v1:
time: 43.7 us; the launch traced here: 43.4 us
  Pallas kernels  39.2 us (90%)
  local copies, waits for them, and re-layouts  3.56 us (8%)
  between operations  0.64 us (1%)
    pallas_call x1, Pallas kernels, on_device(): pl.pallas_call(functools.partial(kernel, rows, cols), out_shape=(jax.Shap...  39.2 us
    unnamed x2, local copies, waits for them, and re-layouts  3.56 us

profile of v1, /device:TPU:1, one launch (start us, length us, event | category | flops | bytes accessed | tf_op | source)
XLA Modules:
  0.0 43.4 jit_solution(15824790674289902163)
XLA Ops:
  0.6 39.2 %coupled_apply.1 = (f32[2048,128]{1,0:T(8,128)}, f32[16,64]{1,0:T(8,128)}) custom-call(f32[2048,128]{1,0:T(8,128)} %bitcast.7, f32[32,128]{1,0:T(8,128)} %bitcast.9, f32[64,1,384]{2,1,0:T(1,128)} %bitcast.8, s32[1,384]{1,0:T(1,128)} %bitcast.10, s32[1,32]{1,0:T(1,128)} %bitcast.11, bf16[2,512,3072]{2,1,0:T(8,128)(2,1)} %matrix_in.1), custom_call_target="tpu_custom_call" | custom-call | tf_op jit(solution)/shard_map/coupled_apply/pallas_call | solution.py:449
  39.8 2.3 %copy.10 = f32[64,4,8,128]{3,2,1,0:T(8,128)} copy(f32[64,4,8,128]{3,2,1,0:T(8,128)} %bitcast.6) | data formatting | bytes 2097152
  42.1 1.3 %copy.11 = f32[16,64]{1,0:T(8,128)} copy(f32[16,64]{1,0:T(8,128)} %get-tuple-element.9) | data formatting | bytes 8192

commit v2 on v1

v2 whole, which is shorter than its diff:
```python
import functools

import jax
import jax.numpy as jnp
from jax import lax
from jax.experimental import pallas as pl
from jax.experimental.pallas import tpu as pltpu
from jax.sharding import PartitionSpec as P

MESH = pl.DeviceIdType.MESH
F32 = jnp.float32
BF16 = jnp.bfloat16
GROUPS = 4


def iota(shape, dim):
    return lax.broadcasted_iota(jnp.int32, shape, dim)


def nt_dot(a, b):
    return lax.dot_general(a, b, (((1,), (1,)), ((), ())), preferred_element_type=F32)


def nn_dot(a, b):
    return lax.dot_general(a, b, (((1,), (0,)), ((), ())), preferred_element_type=F32)


def row_at(me_r, step, rows):
    wide = rows // 2
    if wide == 4:
        third = step % 3
        near = step < 6
        dz = jnp.where(near, step // 3, step - 6)
        dx = jnp.where(near, third + third // 2, 2)
    else:
        dz, dx = step // wide, step % wide
    z = (me_r // wide + dz) % 2
    x = (me_r % wide + dx) % wide
    return z * wide + x


def kernel(
    rows, cols,
    wave_in, medium_in, flux_in, cell_in, target_in, matrix_in,
    volume, boundary_out,
    wave, medium, flux, cell, target, matrix, onehot, picked, unpack, slots, near, relay, traces,
    total, parts, landed,
    faces, edges, faces_in, edges_in, corners_in, faces_f, edges_f, corners_f,
    in_sem, near_send, near_recv, pass_send, pass_recv, own_sem, row_send, row_recv, part_send, part_recv,
    halo_send, halo_recv,
):
    me_r = lax.axis_index("row")
    me_c = lax.axis_index("col")
    comps = wave.shape[0] // 32
    nodes = cell.shape[1]
    slot_len = nodes // cols
    half_slot = slot_len // 2
    span = cols // GROUPS
    mine = me_c // span
    me_n = me_c % span
    after, across, before = [(mine + d) % GROUPS for d in (1, 2, 3)]

    loads = [
        pltpu.make_async_copy(src, dst, in_sem.at[i])
        for i, (src, dst) in enumerate(
            [
                (cell_in, cell),
                (target_in, target),
                (wave_in, wave),
                (flux_in, flux),
                (medium_in, medium),
                (matrix_in, matrix),
            ]
        )
    ]
    for load in loads:
        load.start()

    barrier = pltpu.get_barrier_semaphore()

    def greet(r, c):
        pl.semaphore_signal(barrier, inc=1, device_id=(r, c), device_id_type=MESH)

    greet(me_r, after * span + me_n)
    greet(me_r, before * span + me_n)

    @pl.loop(1, rows)
    def _(i):
        greet((me_r + i) % rows, me_c)

    @pl.loop(1, span)
    def _(i):
        greet(me_r, mine * span + (me_n + i) % span)

    def remote(src, dst, send_sem, recv_sem, r, c):
        return pltpu.make_async_remote_copy(
            src_ref=src,
            dst_ref=dst,
            send_sem=send_sem,
            recv_sem=recv_sem,
            device_id=(r, c),
            device_id_type=MESH,
        )

    loads[0].wait()
    loads[1].wait()
    cells = cell[...]
    place = cells // 128
    onehot[...] = jnp.where(iota((128, nodes), 0) == cells % 128, 1.0, 0.0).astype(BF16)
    node = iota((1, nodes), 1)
    spread = jnp.where(iota((cols, nodes), 0) == iota((cols, nodes), 1) // slot_len, 1.0, 0.0)
    wanted = jnp.broadcast_to(target[...].astype(F32), (8, cols))
    wanted = nn_dot(wanted.astype(BF16), spread.astype(BF16))[:1].astype(jnp.int32)
    within = node % slot_len
    row_of = ((wanted % span) * GROUPS + wanted // span) * 8 + within % half_slot
    lane_half = within // half_slot

    loads[2].wait()
    here = iota((32, nodes), 0) == place

    @pl.loop(0, comps // 8)
    def _(i):
        start = pl.multiple_of(i * 256, 256)
        found = nn_dot(wave[pl.ds(start, 256), :].astype(BF16), onehot[...])
        found = jnp.where(here[None], found.reshape(8, 32, nodes), 0.0)
        found = found.reshape(8, 4, 8, nodes)
        found = (found[:, 0] + found[:, 1]) + (found[:, 2] + found[:, 3])
        picked[pl.ds(pl.multiple_of(i * 64, 64), 64), :] = found.reshape(64, nodes).astype(BF16)

    gather = jnp.where(iota((comps, comps * 8), 0) == iota((comps, comps * 8), 1) // 8, 1.0, 0.0)
    trace = nn_dot(gather.astype(BF16), picked[...])
    blank = jnp.zeros_like(trace)
    sent = None
    for half in range(2):
        match = jnp.logical_and(iota((cols * 8, nodes), 0) == row_of, lane_half == half)
        order = jnp.where(match, 1.0, 0.0).astype(BF16)
        pair = [trace, blank] if half == 0 else [blank, trace]
        term = nt_dot(order, jnp.concatenate(pair, axis=0).astype(BF16))
        sent = term if sent is None else sent + term
    slots[...] = sent.reshape(span, GROUPS, 8, 2 * comps).astype(BF16)

    pl.semaphore_wait(barrier, span - 1 + 2 + rows - 1)

    def near_copy(n, source):
        return remote(
            slots.at[n], near.at[:, source], near_send.at[n], near_recv.at[source], me_r, mine * span + n
        )

    @pl.loop(1, span)
    def _(i):
        near_copy((me_n + span - i) % span, me_n).start()

    own_slots = pltpu.make_async_copy(slots.at[me_n], near.at[:, me_n], near_recv.at[me_n])
    own_slots.start()

    has = [me_c > 0, me_c < cols - 1, me_r > 0, me_r < rows - 1]
    for side in range(2):
        for x in range(4):
            edges[side, x] = wave[pl.ds(x * 8 + side * 7, comps, stride=32), :].astype(BF16)

    def edge_copy(side):
        return remote(
            edges.at[side],
            edges_in.at[1 - side],
            halo_send.at[2 + side],
            halo_recv.at[2 + side],
            me_r + 2 * side - 1,
            me_c,
        )

    for side in range(2):

        @pl.when(has[2 + side])
        def _():
            edge_copy(side).start()

    for side in range(2):

        @pl.loop(0, comps // 8)
        def _(i):
            rows_of = [wave[pl.ds(i * 256 + j * 32 + side * 24, 8), :] for j in range(8)]
            outer = jnp.concatenate(rows_of, axis=0).astype(BF16)
            faces[side, pl.ds(pl.multiple_of(i * 64, 64), 64), :] = outer

    @pl.loop(0, span)
    def _(i):
        near_copy(i, i).wait_recv()

    cut = span // 2

    def whole(g):
        return pl.ds(g * span, span)

    def pass_on(k):
        first, second = (pl.ds(0, cut), pl.ds(cut, span - cut))
        source, target_at, group = [
            (near.at[across, first], relay.at[first], after),
            (near.at[across, second], relay.at[second], before),
            (near.at[after], traces.at[me_r, whole(mine)], after),
            (near.at[before], traces.at[me_r, whole(mine)], before),
            (relay.at[first], traces.at[me_r, pl.ds(before * span, cut)], after),
            (relay.at[second], traces.at[me_r, pl.ds(after * span + cut, span - cut)], before),
        ][k]
        return remote(
            source, target_at, pass_send.at[k], pass_recv.at[k], me_r, group * span + me_n
        )

    def passed(k):
        first, second = (pl.ds(0, cut), pl.ds(cut, span - cut))
        ref, group = [
            (relay.at[first], before),
            (relay.at[second], after),
            (traces.at[me_r, whole(before)], before),
            (traces.at[me_r, whole(after)], after),
            (traces.at[me_r, pl.ds(across * span, cut)], before),
            (traces.at[me_r, pl.ds(across * span + cut, span - cut)], after),
        ][k]
        return remote(ref, ref, pass_send.at[k], pass_recv.at[k], me_r, group * span + me_n)

    halves = [k for k in (0, 1) if k == 1 or cut > 0]
    for k in halves:
        pass_on(k).start()
    pass_on(2).start()
    pass_on(3).start()
    own_group = pltpu.make_async_copy(near.at[mine], traces.at[me_r, whole(mine)], own_sem)
    own_group.start()

    def row_copy(r, g, source):
        return remote(
            source, traces.at[me_r, whole(g)], row_send.at[r, g], row_recv.at[me_r, g], r, me_c
        )

    def row_arrival(r, g):
        ref = traces.at[r, whole(g)]
        return remote(ref, ref, row_send.at[r, g], row_recv.at[r, g], r, me_c)

    def to_rows(g, source):
        @pl.loop(1, rows)
        def _(i):
            row_copy(row_at(me_r, rows - i, rows), g, source).start()

    to_rows(mine, near.at[mine])

    loads[3].wait()

    @pl.loop(0, comps // 8)
    def _(i):
        start = pl.multiple_of(i * 256, 256)
        wide = jnp.where(here[None], flux[pl.ds(i * 8, 8), :, :], 0.0).reshape(256, nodes)
        upper = wide.astype(BF16)
        lower = (wide - upper.astype(F32)).astype(BF16)
        volume[pl.ds(start, 256), :] = nt_dot(upper, onehot[...]) + nt_dot(lower, onehot[...])

    for k in halves:
        passed(k).wait_recv()
        pass_on(4 + k).start()

    def face_copy(side):
        return remote(
            faces.at[side],
            faces_in.at[1 - side],
            halo_send.at[side],
            halo_recv.at[side],
            me_r,
            me_c + 2 * side - 1,
        )

    for side in range(2):

        @pl.when(has[side])
        def _():
            face_copy(side).start()

    for k, g in ((2, before), (3, after)):
        passed(k).wait_recv()
        to_rows(g, traces.at[me_r, whole(g)])

    packed_rows = cols // 2 * 8
    window, shift = nodes * 2 // 3, nodes // 6
    at_row = iota((window, packed_rows), 0)
    packed = iota((window, packed_rows), 1)
    for part in range(2):
        for half in range(2):
            hit = jnp.logical_and(
                at_row - part * shift == (packed // 8) * slot_len + packed % 8 + half * half_slot,
                packed % 8 < half_slot,
            )
            unpack[part, :, half * packed_rows : (half + 1) * packed_rows] = jnp.where(
                hit, 1.0, 0.0
            ).astype(BF16)
    total[...] = jnp.zeros_like(total)

    for k in halves:
        passed(4 + k).wait_recv()
    to_rows(across, traces.at[me_r, whole(across)])

    def corner_copy(side, way):
        return remote(
            edges_in.at[side, 3 * way],
            corners_in.at[2 - 2 * way + side],
            halo_send.at[4 + 2 * side + way],
            halo_recv.at[4 + 2 * side + way],
            me_r,
            me_c + 2 * way - 1,
        )

    for side in range(2):

        @pl.when(has[2 + side])
        def _():
            ref = edges_in.at[side]
            remote(
                ref, ref, halo_send.at[3 - side], halo_recv.at[3 - side], me_r + 2 * side - 1, me_c
            ).wait_recv()
            for way in range(2):

                @pl.when(has[way])
                def _():
                    corner_copy(side, way).start()

    own_group.wait()
    loads[5].wait()
    left = iota((packed_rows, 128), 1) < comps
    minus = iota((packed_rows, 128), 1) % comps < comps // 2
    for late in range(2):
        part = (mine // 2 + late) % 2

        @pl.loop(0, rows)
        def _(step):
            r = row_at(me_r, step, rows)

            @pl.when(step > 0)
            def _():
                row_arrival(r, 2 * part).wait_recv()
                row_arrival(r, 2 * part + 1).wait_recv()

            raw = traces[r, pl.ds(part * (cols // 2), cols // 2)]
            raw = raw.reshape(packed_rows, 2 * comps).astype(F32)
            turned = pltpu.roll(raw, comps, 1)
            stacked = []
            for half in range(2):
                same = jnp.where(left, raw, turned) if half == 0 else jnp.where(left, turned, raw)
                swapped = pltpu.roll(same, comps // 2, 1)
                swapped = jnp.where(minus, -swapped, swapped)
                stacked.append(jnp.concatenate([same, swapped], axis=1).astype(BF16))
            both = nn_dot(unpack[part], jnp.concatenate(stacked, axis=0)).astype(BF16)
            columns = pl.ds(pl.multiple_of(r * nodes + part * (nodes // 3), nodes // 3), window)
            total[...] += nn_dot(matrix[0, :, columns], both[:, :128]) + nn_dot(
                matrix[1, :, columns], both[:, 128:]
            )

    tiles = total[...].reshape(cols, 2, 8, 128)
    parts[...] = jnp.where(
        iota((cols, 8, 128), 2) < comps, tiles[:, 0], tiles[:, 1]
    ).astype(BF16)

    def part_copy(t, source):
        return remote(
            parts.at[t], landed.at[source], part_send.at[t], part_recv.at[source], me_r, t
        )

    for hop in (2, 1, 3, 0):
        first = ((mine + hop) % GROUPS) * span

        @pl.loop(0, span)
        def _(i):
            t = first + i

            @pl.when(t != me_c)
            def _():
                part_copy(t, me_c).start()

    own_part = pltpu.make_async_copy(parts.at[me_c], landed.at[me_c], part_recv.at[me_c])
    own_part.start()

    halos = [
        (faces_in.at[1 - side], faces_f.at[1 - side], side, has[1 - side], (0, 1 - 2 * side))
        for side in range(2)
    ]
    halos += [
        (edges_in.at[side], edges_f.at[side], -1, has[2 + side], None) for side in range(2)
    ]
    halos += [
        (
            corners_in.at[2 - 2 * way + side],
            corners_f.at[2 - 2 * way + side],
            4 + 2 * side + way,
            jnp.logical_and(has[1 - way], has[2 + side]),
            (0, 1 - 2 * way),
        )
        for side in range(2)
        for way in range(2)
    ]
    for got, kept, k, there, step in halos:

        @pl.when(there)
        def _():
            if step is not None:
                remote(
                    got, got, halo_send.at[k], halo_recv.at[k], me_r + step[0], me_c + step[1]
                ).wait_recv()
            kept[...] = got[...].astype(F32)

        @pl.when(jnp.logical_not(there))
        def _():
            kept[...] = jnp.zeros(kept.shape, F32)

    loads[4].wait()
    sublane = iota((8, 128), 0)
    lane = iota((8, 128), 1)

    def depth_sides(v):
        below = jnp.where(lane == 0, 0.0, pltpu.roll(v, 1, 1))
        above = jnp.where(lane == 127, 0.0, pltpu.roll(v, 127, 1))
        return below + above

    def layer(u, low, high):
        below = jnp.where(sublane == 0, jnp.broadcast_to(low, (8, 128)), pltpu.roll(u, 1, 0))
        above = jnp.where(sublane == 7, jnp.broadcast_to(high, (8, 128)), pltpu.roll(u, 7, 0))
        sides = below + above
        outer = depth_sides(sides)
        ring = 2.0 * (sides + depth_sides(u)) + outer
        return u, outer, ring, 4.0 * u + ring

    @pl.loop(0, comps)
    def _(k):
        layers = []
        for x in range(6):
            if x in (0, 5):
                side = 0 if x == 0 else 1
                u = faces_f[side, pl.ds(pl.multiple_of(k * 8, 8), 8), :]
                low = corners_f[2 * side, pl.ds(k, 1), :]
                high = corners_f[2 * side + 1, pl.ds(k, 1), :]
            else:
                u = wave[pl.ds(pl.multiple_of(k * 32 + (x - 1) * 8, 8), 8), :]
                low = edges_f[0, x - 1, pl.ds(k, 1), :]
                high = edges_f[1, x - 1, pl.ds(k, 1), :]
            layers.append(layer(u, low, high))
        for x in range(1, 5):
            u, outer, ring, mass = layers[x]
            stiffness = (8.0 / 3.0) * u - (1.0 / 6.0) * outer
            stiffness -= (1.0 / 12.0) * (layers[x - 1][2] + layers[x + 1][2])
            mass_sum = (2.0 * mass + (layers[x - 1][3] + layers[x + 1][3])) * (1.0 / 27.0)
            where = pl.ds(pl.multiple_of(k * 32 + (x - 1) * 8, 8), 8)
            volume[where, :] = (
                stiffness - medium[pl.ds((x - 1) * 8, 8), :] * mass_sum - volume[where, :]
            )

    @pl.loop(1, span)
    def _(i):
        near_copy((me_n + i) % span, me_n).wait_send()

    for k in halves:
        pass_on(k).wait_send()
        pass_on(4 + k).wait_send()
    pass_on(2).wait_send()
    pass_on(3).wait_send()

    @pl.loop(1, rows)
    def _(i):
        @pl.loop(0, GROUPS)
        def _(g):
            row_copy((me_r + i) % rows, g, traces.at[me_r, whole(g)]).wait_send()

    for side in range(2):

        @pl.when(has[side])
        def _():
            face_copy(side).wait_send()

        @pl.when(has[2 + side])
        def _():
            edge_copy(side).wait_send()
            for way in range(2):

                @pl.when(has[way])
                def _():
                    corner_copy(side, way).wait_send()

    @pl.loop(0, cols)
    def _(c):
        part_copy(c, c).wait_recv()

    sums = jnp.sum(landed[...].astype(F32), axis=0)
    boundary_out[0:8, :] = sums[:, :comps]
    boundary_out[8:16, :] = pltpu.roll(sums, comps, 1)[:, :comps]

    @pl.loop(0, cols)
    def _(t):
        @pl.when(t != me_c)
        def _():
            part_copy(t, me_c).wait_send()


def on_device(rows, cols, wave_field, medium_term, node_flux, node_cell, block_target, boundary_matrix):
    comps = wave_field.shape[0]
    nodes = node_cell.shape[-1]
    slab_rows, width = boundary_matrix.shape[1:]
    own_rows = slab_rows // cols
    vmem = pltpu.VMEM
    dma = pltpu.SemaphoreType.DMA
    volume, boundary = pl.pallas_call(
        functools.partial(kernel, rows, cols),
        out_shape=(
            pltpu.VMEM((comps * 32, 128), F32),
            pltpu.VMEM((own_rows, comps), F32),
        ),
        in_specs=[pl.BlockSpec(memory_space=pltpu.HBM)] * 6,
        out_specs=(pl.BlockSpec(memory_space=pltpu.VMEM), pl.BlockSpec(memory_space=pltpu.VMEM)),
        scratch_shapes=[
            vmem((comps * 32, 128), F32),
            vmem((32, 128), F32),
            vmem((comps, 1, nodes), F32),
            vmem((1, nodes), jnp.int32),
            vmem((1, cols), jnp.int32),
            vmem((2, slab_rows, width), BF16),
            vmem((128, nodes), BF16),
            vmem((comps * 8, nodes), BF16),
            vmem((2, nodes * 2 // 3, cols * 8), BF16),
            vmem((cols // GROUPS, GROUPS, 8, 128), BF16),
            vmem((GROUPS, cols // GROUPS, 8, 128), BF16),
            vmem((cols // GROUPS, 8, 128), BF16),
            vmem((rows, cols, 8, 128), BF16),
            vmem((slab_rows, 128), F32),
            vmem((cols, 8, 128), BF16),
            vmem((cols, 8, 128), BF16),
            vmem((2, comps * 8, 128), BF16),
            vmem((2, 4, comps, 128), BF16),
            vmem((2, comps * 8, 128), BF16),
            vmem((2, 4, comps, 128), BF16),
            vmem((4, comps, 128), BF16),
            vmem((2, comps * 8, 128), F32),
            vmem((2, 4, comps, 128), F32),
            vmem((4, comps, 128), F32),
            dma((6,)),
            dma((cols // GROUPS,)),
            dma((cols // GROUPS,)),
            dma((6,)),
            dma((6,)),
            dma(()),
            dma((rows, GROUPS)),
            dma((rows, GROUPS)),
            dma((cols,)),
            dma((cols,)),
            dma((8,)),
            dma((8,)),
        ],
        compiler_params=pltpu.CompilerParams(
            collective_id=0, has_side_effects=True, vmem_limit_bytes=48 * 2**20
        ),
        name="coupled_apply",
    )(
        *[
            pltpu.with_memory_space_constraint(x, pltpu.HBM)
            for x in (
                wave_field.reshape(comps * 32, 128),
                medium_term.reshape(32, 128),
                node_flux.reshape(comps, 1, nodes),
                node_cell.reshape(1, nodes),
                block_target.reshape(1, cols),
                boundary_matrix,
            )
        ]
    )
    return volume.reshape(wave_field.shape), boundary


def solution(mesh):
    in_specs = (
        P(None, "col", "row", None),
        P("col", "row", None),
        P(None, "col", "row", None),
        P("col", "row", None),
        P("col", "row", None),
        P(None, "row", "col"),
    )
    out_specs = (P(None, "col", "row", None), P(("row", "col"), None))
    return jax.shard_map(
        functools.partial(on_device, mesh.shape["row"], mesh.shape["col"]),
        mesh=mesh,
        in_specs=in_specs,
        out_specs=out_specs,
        check_vma=False,
    )
```

time: 43.7 us -> 43.1 us (0.986)
  local copies, waits for them, and re-layouts: 3.56 us -> 1.57 us
  Pallas kernels: 39.2 us -> 40.5 us
    unnamed x2, local copies, waits for them, and re-layouts: 3.56 us -> 1.57 us
    pallas_call x1, Pallas kernels: 39.2 us -> 40.5 us  [on_device(): pl.pallas_call(functools.partial(kernel, rows, cols), out_shape=(pltpu.VM...]
where the time goes in v2:
time: 43.1 us; the launch traced here: 42.7 us
  Pallas kernels  40.5 us (94%)
  local copies, waits for them, and re-layouts  1.57 us (4%)
  between operations  0.64 us (1%)
    pallas_call x1, Pallas kernels, on_device(): pl.pallas_call(functools.partial(kernel, rows, cols), out_shape=(pltpu.VM...  40.5 us
    unnamed x2, local copies, waits for them, and re-layouts  1.57 us

profile of v2, /device:TPU:1, one launch (start us, length us, event | category | flops | bytes accessed | tf_op | source)
XLA Modules:
  0.0 42.7 jit_solution(15731345259876145859)
XLA Ops:
  0.6 40.5 %coupled_apply.1 = (f32[2048,128]{1,0:T(8,128)S(1)}, f32[16,64]{1,0:T(8,128)S(1)}) custom-call(f32[2048,128]{1,0:T(8,128)} %bitcast.7, f32[32,128]{1,0:T(8,128)} %bitcast.9, f32[64,1,384]{2,1,0:T(1,128)} %bitcast.8, s32[1,384]{1,0:T(1,128)} %bitcast.10, s32[1,32]{1,0:T(1,128)} %bitcast.11, bf16[2,512,3072]{2,1,0:T(8,128)(2,1)} %matrix_in.1), custom_call_target="tpu_custom_call" | custom-call | tf_op jit(solution)/shard_map/coupled_apply/pallas_call | solution.py:502
  41.1 1.0 %copy.10 = f32[64,4,8,128]{3,2,1,0:T(8,128)} copy(f32[64,4,8,128]{3,2,1,0:T(8,128)S(1)} %bitcast.6) | data formatting | bytes 2097152
  42.1 0.6 %copy.11 = f32[16,64]{1,0:T(8,128)} copy(f32[16,64]{1,0:T(8,128)S(1)} %get-tuple-element.7) | data formatting | bytes 8192

commit v3 on v2

--- a/solution.py
+++ b/solution.py
@@ -25,25 +25,11 @@
     return lax.dot_general(a, b, (((1,), (0,)), ((), ())), preferred_element_type=F32)
 
 
-def row_at(me_r, step, rows):
-    wide = rows // 2
-    if wide == 4:
-        third = step % 3
-        near = step < 6
-        dz = jnp.where(near, step // 3, step - 6)
-        dx = jnp.where(near, third + third // 2, 2)
-    else:
-        dz, dx = step // wide, step % wide
-    z = (me_r // wide + dz) % 2
-    x = (me_r % wide + dx) % wide
-    return z * wide + x
-
-
 def kernel(
     rows, cols,
     wave_in, medium_in, flux_in, cell_in, target_in, matrix_in,
     volume, boundary_out,
-    wave, medium, flux, cell, target, matrix, onehot, picked, unpack, slots, near, relay, traces,
+    wave, medium, flux, cell, target, matrix, onehot, picked, unpack, placed, slots, near, relay, traces,
     total, parts, landed,
     faces, edges, faces_in, edges_in, corners_in, faces_f, edges_f, corners_f,
     in_sem, near_send, near_recv, pass_send, pass_recv, own_sem, row_send, row_recv, part_send, part_recv,
@@ -143,14 +129,14 @@
 
     def near_copy(n, source):
         return remote(
-            slots.at[n], near.at[:, source], near_send.at[n], near_recv.at[source], me_r, mine * span + n
+            slots.at[n], near.at[:, source], near_send, near_recv, me_r, mine * span + n
         )
 
     @pl.loop(1, span)
     def _(i):
         near_copy((me_n + span - i) % span, me_n).start()
 
-    own_slots = pltpu.make_async_copy(slots.at[me_n], near.at[:, me_n], near_recv.at[me_n])
+    own_slots = pltpu.make_async_copy(slots.at[me_n], near.at[:, me_n], near_recv)
     own_slots.start()
 
     has = [me_c > 0, me_c < cols - 1, me_r > 0, me_r < rows - 1]
@@ -182,9 +168,7 @@
             outer = jnp.concatenate(rows_of, axis=0).astype(BF16)
             faces[side, pl.ds(pl.multiple_of(i * 64, 64), 64), :] = outer
 
-    @pl.loop(0, span)
-    def _(i):
-        near_copy(i, i).wait_recv()
+    remote(near, near, near_send, near_recv, me_r, after * span + me_n).wait_recv()
 
     cut = span // 2
 
@@ -225,21 +209,50 @@
     own_group = pltpu.make_async_copy(near.at[mine], traces.at[me_r, whole(mine)], own_sem)
     own_group.start()
 
-    def row_copy(r, g, source):
+    wide = rows // 2
+
+    def row_at(dz, dx):
+        return (me_r // wide + dz) % 2 * wide + (me_r % wide + dx) % wide
+
+    across_x = wide // 2
+    steps = [(0, across_x), (0, 1), (0, wide - 1), (1, 0)] if wide > 1 else [(1, 0)]
+    far_steps = [(1, across_x), (1, 1), (1, wide - 1)] if wide > 1 else []
+    plane, opposite = row_at(1, 0), row_at(0, across_x)
+
+    def row_copy(k, step, g, r, source):
         return remote(
-            source, traces.at[me_r, whole(g)], row_send.at[r, g], row_recv.at[me_r, g], r, me_c
+            source, traces.at[r, whole(g)], row_send.at[k, g], row_recv.at[r, g], row_at(*step), me_c
         )
 
     def row_arrival(r, g):
         ref = traces.at[r, whole(g)]
-        return remote(ref, ref, row_send.at[r, g], row_recv.at[r, g], r, me_c)
-
-    def to_rows(g, source):
-        @pl.loop(1, rows)
-        def _(i):
-            row_copy(row_at(me_r, rows - i, rows), g, source).start()
-
-    to_rows(mine, near.at[mine])
+        return remote(ref, ref, row_send.at[0, g], row_recv.at[r, g], plane, me_c)
+
+    def first_hops(g, source):
+        return [row_copy(k, step, g, me_r, source) for k, step in enumerate(steps)]
+
+    def second_hops(g, first, last):
+        sends = [(4, (0, 1), plane), (5, (0, wide - 1), plane), (6, (1, 0), opposite)]
+        return [
+            row_copy(k, step, g, r, traces.at[r, whole(g)])
+            for k, step, r in (sends[first:last] if wide > 1 else [])
+        ]
+
+    def far_hops(g, source):
+        return [row_copy(4 + k, step, g, me_r, source) for k, step in enumerate(far_steps)]
+
+    def go(copies):
+        for copy in copies:
+            copy.start()
+
+    def go_on(g):
+        if wide > 1:
+            row_arrival(plane, g).wait_recv()
+            go(second_hops(g, 0, 2))
+            row_arrival(opposite, g).wait_recv()
+            go(second_hops(g, 2, 3))
+
+    go(first_hops(mine, near.at[mine]))
 
     loads[3].wait()
 
@@ -255,25 +268,11 @@
         passed(k).wait_recv()
         pass_on(4 + k).start()
 
-    def face_copy(side):
-        return remote(
-            faces.at[side],
-            faces_in.at[1 - side],
-            halo_send.at[side],
-            halo_recv.at[side],
-            me_r,
-            me_c + 2 * side - 1,
-        )
-
-    for side in range(2):
-
-        @pl.when(has[side])
-        def _():
-            face_copy(side).start()
-
     for k, g in ((2, before), (3, after)):
         passed(k).wait_recv()
-        to_rows(g, traces.at[me_r, whole(g)])
+        go(first_hops(g, traces.at[me_r, whole(g)]))
+
+    go_on(mine)
 
     packed_rows = cols // 2 * 8
     window, shift = nodes * 2 // 3, nodes // 6
@@ -292,7 +291,26 @@
 
     for k in halves:
         passed(4 + k).wait_recv()
-    to_rows(across, traces.at[me_r, whole(across)])
+    go(far_hops(across, traces.at[me_r, whole(across)]))
+    go(first_hops(across, traces.at[me_r, whole(across)]))
+    go_on(before)
+    go_on(after)
+
+    def face_copy(side):
+        return remote(
+            faces.at[side],
+            faces_in.at[1 - side],
+            halo_send.at[side],
+            halo_recv.at[side],
+            me_r,
+            me_c + 2 * side - 1,
+        )
+
+    for side in range(2):
+
+        @pl.when(has[side])
+        def _():
+            face_copy(side).start()
 
     def corner_copy(side, way):
         return remote(
@@ -322,18 +340,23 @@
     loads[5].wait()
     left = iota((packed_rows, 128), 1) < comps
     minus = iota((packed_rows, 128), 1) % comps < comps // 2
+    slab = matrix.shape[1]
     for late in range(2):
         part = (mine // 2 + late) % 2
 
-        @pl.loop(0, rows)
-        def _(step):
-            r = row_at(me_r, step, rows)
-
-            @pl.when(step > 0)
-            def _():
-                row_arrival(r, 2 * part).wait_recv()
-                row_arrival(r, 2 * part + 1).wait_recv()
-
+        def arrivals(step, g):
+            row_arrival(row_at(*step), g).wait_recv()
+
+        for step in steps + far_steps:
+            if late:
+                arrivals(step, across)
+                if step not in ((1, 0), (0, across_x)) or wide == 1:
+                    arrivals(step, jnp.where(mine % 2 == 0, before, after))
+            elif step not in ((1, 0), (0, across_x)) or wide == 1:
+                arrivals(step, mine)
+                arrivals(step, jnp.where(mine % 2 == 0, after, before))
+
+        for r in range(rows):
             raw = traces[r, pl.ds(part * (cols // 2), cols // 2)]
             raw = raw.reshape(packed_rows, 2 * comps).astype(F32)
             turned = pltpu.roll(raw, comps, 1)
@@ -343,11 +366,21 @@
                 swapped = pltpu.roll(same, comps // 2, 1)
                 swapped = jnp.where(minus, -swapped, swapped)
                 stacked.append(jnp.concatenate([same, swapped], axis=1).astype(BF16))
-            both = nn_dot(unpack[part], jnp.concatenate(stacked, axis=0)).astype(BF16)
-            columns = pl.ds(pl.multiple_of(r * nodes + part * (nodes // 3), nodes // 3), window)
-            total[...] += nn_dot(matrix[0, :, columns], both[:, :128]) + nn_dot(
-                matrix[1, :, columns], both[:, 128:]
-            )
+            both = nn_dot(unpack[part], jnp.concatenate(stacked, axis=0))
+            placed[r] = both.astype(BF16)
+
+        @pl.loop(0, 2)
+        def _(i):
+            upright = pl.ds(pl.multiple_of(i * (slab // 2), slab // 2), slab // 2)
+            terms = total[upright, :]
+            for r in range(rows):
+                at = r * nodes + part * (nodes // 3)
+                columns = pl.ds(pl.multiple_of(at, nodes // 3), window)
+                for half in range(2):
+                    terms += nn_dot(
+                        matrix[half, upright, columns], placed[r, :, half * 128 : half * 128 + 128]
+                    )
+            total[upright, :] = terms
 
     tiles = total[...].reshape(cols, 2, 8, 128)
     parts[...] = jnp.where(
@@ -356,7 +389,7 @@
 
     def part_copy(t, source):
         return remote(
-            parts.at[t], landed.at[source], part_send.at[t], part_recv.at[source], me_r, t
+            parts.at[t], landed.at[source], part_send, part_recv, me_r, t
         )
 
     for hop in (2, 1, 3, 0):
@@ -370,7 +403,7 @@
             def _():
                 part_copy(t, me_c).start()
 
-    own_part = pltpu.make_async_copy(parts.at[me_c], landed.at[me_c], part_recv.at[me_c])
+    own_part = pltpu.make_async_copy(parts.at[me_c], landed.at[me_c], part_recv)
     own_part.start()
 
     halos = [
@@ -422,7 +455,7 @@
         ring = 2.0 * (sides + depth_sides(u)) + outer
         return u, outer, ring, 4.0 * u + ring
 
-    @pl.loop(0, comps)
+    @pl.loop(0, comps, unroll=4)
     def _(k):
         layers = []
         for x in range(6):
@@ -446,9 +479,9 @@
                 stiffness - medium[pl.ds((x - 1) * 8, 8), :] * mass_sum - volume[where, :]
             )
 
-    @pl.loop(1, span)
-    def _(i):
-        near_copy((me_n + i) % span, me_n).wait_send()
+    if span > 1:
+        others = slots.at[pl.ds(0, span - 1)]
+        remote(others, others, near_send, near_recv, me_r, after * span + me_n).wait_send()
 
     for k in halves:
         pass_on(k).wait_send()
@@ -456,11 +489,14 @@
     pass_on(2).wait_send()
     pass_on(3).wait_send()
 
-    @pl.loop(1, rows)
-    def _(i):
-        @pl.loop(0, GROUPS)
-        def _(g):
-            row_copy((me_r + i) % rows, g, traces.at[me_r, whole(g)]).wait_send()
+    for g in (mine, before, after, across):
+        for copy in first_hops(g, traces.at[me_r, whole(g)]):
+            copy.wait_send()
+    for g in (mine, before, after):
+        for copy in second_hops(g, 0, 3):
+            copy.wait_send()
+    for copy in far_hops(across, traces.at[me_r, whole(across)]):
+        copy.wait_send()
 
     for side in range(2):
 
@@ -477,19 +513,14 @@
                 def _():
                     corner_copy(side, way).wait_send()
 
-    @pl.loop(0, cols)
-    def _(c):
-        part_copy(c, c).wait_recv()
+    remote(landed, landed, part_send, part_recv, me_r, after * span + me_n).wait_recv()
 
     sums = jnp.sum(landed[...].astype(F32), axis=0)
     boundary_out[0:8, :] = sums[:, :comps]
     boundary_out[8:16, :] = pltpu.roll(sums, comps, 1)[:, :comps]
 
-    @pl.loop(0, cols)
-    def _(t):
-        @pl.when(t != me_c)
-        def _():
-            part_copy(t, me_c).wait_send()
+    others = parts.at[pl.ds(0, cols - 1)]
+    remote(others, others, part_send, part_recv, me_r, after * span + me_n).wait_send()
 
 
 def on_device(rows, cols, wave_field, medium_term, node_flux, node_cell, block_target, boundary_matrix):
@@ -517,6 +548,7 @@
             vmem((128, nodes), BF16),
             vmem((comps * 8, nodes), BF16),
             vmem((2, nodes * 2 // 3, cols * 8), BF16),
+            vmem((rows, nodes * 2 // 3, 256), BF16),
             vmem((cols // GROUPS, GROUPS, 8, 128), BF16),
             vmem((GROUPS, cols // GROUPS, 8, 128), BF16),
             vmem((cols // GROUPS, 8, 128), BF16),
@@ -533,15 +565,15 @@
             vmem((2, 4, comps, 128), F32),
             vmem((4, comps, 128), F32),
             dma((6,)),
-            dma((cols // GROUPS,)),
-            dma((cols // GROUPS,)),
+            dma(()),
+            dma(()),
             dma((6,)),
             dma((6,)),
             dma(()),
+            dma((7, GROUPS)),
             dma((rows, GROUPS)),
-            dma((rows, GROUPS)),
-            dma((cols,)),
-            dma((cols,)),
+            dma(()),
+            dma(()),
             dma((8,)),
             dma((8,)),
         ],

time: 43.1 us -> 38.4 us (0.89)
  Pallas kernels: 40.5 us -> 36.1 us
    pallas_call x1, Pallas kernels: 40.5 us -> 36.1 us  [on_device(): pl.pallas_call(functools.partial(kernel, rows, cols), out_shape=(pltpu.VM...]
where the time goes in v3:
time: 38.4 us; the launch traced here: 38.3 us
  Pallas kernels  36.1 us (94%)
  local copies, waits for them, and re-layouts  1.57 us (4%)
  between operations  0.64 us (2%)
    pallas_call x1, Pallas kernels, on_device(): pl.pallas_call(functools.partial(kernel, rows, cols), out_shape=(pltpu.VM...  36.1 us
    unnamed x2, local copies, waits for them, and re-layouts  1.57 us

profile of v3, /device:TPU:1, one launch (start us, length us, event | category | flops | bytes accessed | tf_op | source)
XLA Modules:
  0.0 38.3 jit_solution(17554767970135099367)
XLA Ops:
  0.6 36.1 %coupled_apply.1 = (f32[2048,128]{1,0:T(8,128)S(1)}, f32[16,64]{1,0:T(8,128)S(1)}) custom-call(f32[2048,128]{1,0:T(8,128)} %bitcast.7, f32[32,128]{1,0:T(8,128)} %bitcast.9, f32[64,1,384]{2,1,0:T(1,128)} %bitcast.8, s32[1,384]{1,0:T(1,128)} %bitcast.10, s32[1,32]{1,0:T(1,128)} %bitcast.11, bf16[2,512,3072]{2,1,0:T(8,128)(2,1)} %matrix_in.1), custom_call_target="tpu_custom_call" | custom-call | tf_op jit(solution)/shard_map/coupled_apply/pallas_call | solution.py:533
  36.8 1.0 %copy.10 = f32[64,4,8,128]{3,2,1,0:T(8,128)} copy(f32[64,4,8,128]{3,2,1,0:T(8,128)S(1)} %bitcast.6) | data formatting | bytes 2097152
  37.7 0.6 %copy.11 = f32[16,64]{1,0:T(8,128)} copy(f32[16,64]{1,0:T(8,128)S(1)} %get-tuple-element.7) | data formatting | bytes 8192

commit v4 on v3

--- a/solution.py
+++ b/solution.py
@@ -29,10 +29,10 @@
     rows, cols,
     wave_in, medium_in, flux_in, cell_in, target_in, matrix_in,
     volume, boundary_out,
-    wave, medium, flux, cell, target, matrix, onehot, picked, unpack, placed, slots, near, relay, traces,
+    wave, medium, flux, cell, target, matrix, onehot, picked, order_of, placed, slots, near, outgoing, traces,
     total, parts, landed,
     faces, edges, faces_in, edges_in, corners_in, faces_f, edges_f, corners_f,
-    in_sem, near_send, near_recv, pass_send, pass_recv, own_sem, row_send, row_recv, part_send, part_recv,
+    in_sem, ready, near_send, near_recv, pass_send, pass_recv, row_send, row_recv, part_send, part_recv,
     halo_send, halo_recv,
 ):
     me_r = lax.axis_index("row")
@@ -104,7 +104,7 @@
     loads[2].wait()
     here = iota((32, nodes), 0) == place
 
-    @pl.loop(0, comps // 8)
+    @pl.loop(0, comps // 8, unroll=2)
     def _(i):
         start = pl.multiple_of(i * 256, 256)
         found = nn_dot(wave[pl.ds(start, 256), :].astype(BF16), onehot[...])
@@ -127,6 +127,11 @@
 
     pl.semaphore_wait(barrier, span - 1 + 2 + rows - 1)
 
+    for group in (after, before):
+        pl.semaphore_signal(
+            ready, inc=1, device_id=(me_r, group * span + me_n), device_id_type=MESH
+        )
+
     def near_copy(n, source):
         return remote(
             slots.at[n], near.at[:, source], near_send, near_recv, me_r, mine * span + n
@@ -168,46 +173,49 @@
             outer = jnp.concatenate(rows_of, axis=0).astype(BF16)
             faces[side, pl.ds(pl.multiple_of(i * 64, 64), 64), :] = outer
 
+    group_half = span * half_slot
+    at_row = iota((2 * group_half, span * 16), 0)
+    packed = iota((2 * group_half, span * 16), 1)
+    turned_in = packed // (span * 8)
+    upper_out = at_row // group_half
+    from_node = packed % (span * 8) // 8 * slot_len + packed % 8
+    from_node += jnp.where(turned_in == upper_out, 0, half_slot)
+    hit = jnp.logical_and(from_node == at_row, packed % 8 < half_slot)
+    order_of[...] = jnp.where(hit, 1.0, 0.0).astype(BF16)
     remote(near, near, near_send, near_recv, me_r, after * span + me_n).wait_recv()
 
-    cut = span // 2
-
-    def whole(g):
-        return pl.ds(g * span, span)
+    raw = [near[g].reshape(span * 8, 2 * comps) for g in range(GROUPS)]
+    turned = [pltpu.roll(block.astype(F32), comps, 1).astype(BF16) for block in raw]
+    stacks = [jnp.concatenate(pair, axis=0) for pair in zip(raw, turned)]
+    found = nn_dot(order_of[...], jnp.concatenate(stacks, axis=1))
+    found = jnp.where(
+        iota((group_half, GROUPS * 128), 1) % 128 < comps, found[:group_half], found[group_half:]
+    )
+    piece = outgoing.shape[1:]
+    for g in range(GROUPS):
+        outgoing[g] = found[:, g * 128 : g * 128 + 128].reshape(piece).astype(BF16)
+
+    beside = [across, after, before]
 
     def pass_on(k):
-        first, second = (pl.ds(0, cut), pl.ds(cut, span - cut))
-        source, target_at, group = [
-            (near.at[across, first], relay.at[first], after),
-            (near.at[across, second], relay.at[second], before),
-            (near.at[after], traces.at[me_r, whole(mine)], after),
-            (near.at[before], traces.at[me_r, whole(mine)], before),
-            (relay.at[first], traces.at[me_r, pl.ds(before * span, cut)], after),
-            (relay.at[second], traces.at[me_r, pl.ds(after * span + cut, span - cut)], before),
-        ][k]
         return remote(
-            source, target_at, pass_send.at[k], pass_recv.at[k], me_r, group * span + me_n
+            outgoing.at[beside[k]],
+            traces.at[me_r, mine],
+            pass_send.at[k],
+            pass_recv.at[k],
+            me_r,
+            beside[k] * span + me_n,
         )
 
     def passed(k):
-        first, second = (pl.ds(0, cut), pl.ds(cut, span - cut))
-        ref, group = [
-            (relay.at[first], before),
-            (relay.at[second], after),
-            (traces.at[me_r, whole(before)], before),
-            (traces.at[me_r, whole(after)], after),
-            (traces.at[me_r, pl.ds(across * span, cut)], before),
-            (traces.at[me_r, pl.ds(across * span + cut, span - cut)], after),
-        ][k]
+        group = [across, before, after][k]
+        ref = traces.at[me_r, group]
         return remote(ref, ref, pass_send.at[k], pass_recv.at[k], me_r, group * span + me_n)
 
-    halves = [k for k in (0, 1) if k == 1 or cut > 0]
-    for k in halves:
+    pl.semaphore_wait(ready, 2)
+    for k in range(3):
         pass_on(k).start()
-    pass_on(2).start()
-    pass_on(3).start()
-    own_group = pltpu.make_async_copy(near.at[mine], traces.at[me_r, whole(mine)], own_sem)
-    own_group.start()
+    traces[me_r, mine] = outgoing[mine]
 
     wide = rows // 2
 
@@ -219,27 +227,23 @@
     far_steps = [(1, across_x), (1, 1), (1, wide - 1)] if wide > 1 else []
     plane, opposite = row_at(1, 0), row_at(0, across_x)
 
-    def row_copy(k, step, g, r, source):
-        return remote(
-            source, traces.at[r, whole(g)], row_send.at[k, g], row_recv.at[r, g], row_at(*step), me_c
-        )
+    def row_copy(k, step, g, r):
+        ref = traces.at[r, g]
+        return remote(ref, ref, row_send.at[k, g], row_recv.at[r, g], row_at(*step), me_c)
 
     def row_arrival(r, g):
-        ref = traces.at[r, whole(g)]
+        ref = traces.at[r, g]
         return remote(ref, ref, row_send.at[0, g], row_recv.at[r, g], plane, me_c)
 
-    def first_hops(g, source):
-        return [row_copy(k, step, g, me_r, source) for k, step in enumerate(steps)]
+    def first_hops(g):
+        return [row_copy(k, step, g, me_r) for k, step in enumerate(steps)]
 
     def second_hops(g, first, last):
         sends = [(4, (0, 1), plane), (5, (0, wide - 1), plane), (6, (1, 0), opposite)]
-        return [
-            row_copy(k, step, g, r, traces.at[r, whole(g)])
-            for k, step, r in (sends[first:last] if wide > 1 else [])
-        ]
-
-    def far_hops(g, source):
-        return [row_copy(4 + k, step, g, me_r, source) for k, step in enumerate(far_steps)]
+        return [row_copy(k, step, g, r) for k, step, r in (sends[first:last] if wide > 1 else [])]
+
+    def far_hops(g):
+        return [row_copy(4 + k, step, g, me_r) for k, step in enumerate(far_steps)]
 
     def go(copies):
         for copy in copies:
@@ -252,11 +256,11 @@
             row_arrival(opposite, g).wait_recv()
             go(second_hops(g, 2, 3))
 
-    go(first_hops(mine, near.at[mine]))
+    go(first_hops(mine))
 
     loads[3].wait()
 
-    @pl.loop(0, comps // 8)
+    @pl.loop(0, comps // 8, unroll=2)
     def _(i):
         start = pl.multiple_of(i * 256, 256)
         wide = jnp.where(here[None], flux[pl.ds(i * 8, 8), :, :], 0.0).reshape(256, nodes)
@@ -264,35 +268,15 @@
         lower = (wide - upper.astype(F32)).astype(BF16)
         volume[pl.ds(start, 256), :] = nt_dot(upper, onehot[...]) + nt_dot(lower, onehot[...])
 
-    for k in halves:
+    for k, g in ((1, before), (2, after)):
         passed(k).wait_recv()
-        pass_on(4 + k).start()
-
-    for k, g in ((2, before), (3, after)):
-        passed(k).wait_recv()
-        go(first_hops(g, traces.at[me_r, whole(g)]))
-
+        go(first_hops(g))
+
+    total[...] = jnp.zeros_like(total)
     go_on(mine)
-
-    packed_rows = cols // 2 * 8
-    window, shift = nodes * 2 // 3, nodes // 6
-    at_row = iota((window, packed_rows), 0)
-    packed = iota((window, packed_rows), 1)
-    for part in range(2):
-        for half in range(2):
-            hit = jnp.logical_and(
-                at_row - part * shift == (packed // 8) * slot_len + packed % 8 + half * half_slot,
-                packed % 8 < half_slot,
-            )
-            unpack[part, :, half * packed_rows : (half + 1) * packed_rows] = jnp.where(
-                hit, 1.0, 0.0
-            ).astype(BF16)
-    total[...] = jnp.zeros_like(total)
-
-    for k in halves:
-        passed(4 + k).wait_recv()
-    go(far_hops(across, traces.at[me_r, whole(across)]))
-    go(first_hops(across, traces.at[me_r, whole(across)]))
+    passed(0).wait_recv()
+    go(far_hops(across))
+    go(first_hops(across))
     go_on(before)
     go_on(after)
 
@@ -336,11 +320,9 @@
                 def _():
                     corner_copy(side, way).start()
 
-    own_group.wait()
     loads[5].wait()
-    left = iota((packed_rows, 128), 1) < comps
-    minus = iota((packed_rows, 128), 1) % comps < comps // 2
     slab = matrix.shape[1]
+    window, shift = nodes * 2 // 3, nodes // 6
     for late in range(2):
         part = (mine // 2 + late) % 2
 
@@ -357,35 +339,40 @@
                 arrivals(step, jnp.where(mine % 2 == 0, after, before))
 
         for r in range(rows):
-            raw = traces[r, pl.ds(part * (cols // 2), cols // 2)]
-            raw = raw.reshape(packed_rows, 2 * comps).astype(F32)
-            turned = pltpu.roll(raw, comps, 1)
-            stacked = []
-            for half in range(2):
-                same = jnp.where(left, raw, turned) if half == 0 else jnp.where(left, turned, raw)
-                swapped = pltpu.roll(same, comps // 2, 1)
-                swapped = jnp.where(minus, -swapped, swapped)
-                stacked.append(jnp.concatenate([same, swapped], axis=1).astype(BF16))
-            both = nn_dot(unpack[part], jnp.concatenate(stacked, axis=0))
-            placed[r] = both.astype(BF16)
+            pieces = []
+            for g in range(2):
+                block = traces[r, 2 * part + g].astype(F32).reshape(group_half, 2 * comps)
+                pieces += [block, pltpu.roll(block, comps, 1)]
+            placed[r, pl.ds(pl.multiple_of(part * shift, shift), nodes // 2), :] = jnp.concatenate(
+                pieces, axis=0
+            ).astype(BF16)
+            placed[r, pl.ds(pl.multiple_of((1 - part) * (nodes // 2), shift), shift), :] = (
+                jnp.zeros((shift, 128), BF16)
+            )
 
         @pl.loop(0, 2)
         def _(i):
             upright = pl.ds(pl.multiple_of(i * (slab // 2), slab // 2), slab // 2)
-            terms = total[upright, :]
-            for r in range(rows):
-                at = r * nodes + part * (nodes // 3)
-                columns = pl.ds(pl.multiple_of(at, nodes // 3), window)
-                for half in range(2):
-                    terms += nn_dot(
-                        matrix[half, upright, columns], placed[r, :, half * 128 : half * 128 + 128]
-                    )
-            total[upright, :] = terms
-
-    tiles = total[...].reshape(cols, 2, 8, 128)
-    parts[...] = jnp.where(
-        iota((cols, 8, 128), 2) < comps, tiles[:, 0], tiles[:, 1]
-    ).astype(BF16)
+            for half in range(2):
+                terms = total[half, upright, :]
+                for r in range(rows):
+                    at = r * nodes + part * (nodes // 3)
+                    columns = pl.ds(pl.multiple_of(at, nodes // 3), window)
+                    terms += nn_dot(matrix[half, upright, columns], placed[r])
+                total[half, upright, :] = terms
+
+    lower = iota((cols * 8, 128), 1) < comps
+    minus = iota((cols * 8, 128), 1) % comps < comps // 2
+    folded = []
+    for half in range(2):
+        tiles = total[half].reshape(cols, 2, 8, 128)
+        first, second = [tiles[:, i].reshape(cols * 8, 128) for i in range(2)]
+        folded.append(jnp.where(lower, first, pltpu.roll(second, comps, 1)))
+    real, imag = folded
+    imag = jnp.where(
+        minus, -pltpu.roll(imag, 128 - comps // 2, 1), pltpu.roll(imag, comps // 2, 1)
+    )
+    parts[...] = (real + imag).reshape(cols, 8, 128).astype(BF16)
 
     def part_copy(t, source):
         return remote(
@@ -483,19 +470,16 @@
         others = slots.at[pl.ds(0, span - 1)]
         remote(others, others, near_send, near_recv, me_r, after * span + me_n).wait_send()
 
-    for k in halves:
+    for k in range(3):
         pass_on(k).wait_send()
-        pass_on(4 + k).wait_send()
-    pass_on(2).wait_send()
-    pass_on(3).wait_send()
 
     for g in (mine, before, after, across):
-        for copy in first_hops(g, traces.at[me_r, whole(g)]):
+        for copy in first_hops(g):
             copy.wait_send()
     for g in (mine, before, after):
         for copy in second_hops(g, 0, 3):
             copy.wait_send()
-    for copy in far_hops(across, traces.at[me_r, whole(across)]):
+    for copy in far_hops(across):
         copy.wait_send()
 
     for side in range(2):
@@ -528,6 +512,8 @@
     nodes = node_cell.shape[-1]
     slab_rows, width = boundary_matrix.shape[1:]
     own_rows = slab_rows // cols
+    group_half = nodes // GROUPS // 2
+    pieces = 6 if group_half % 48 == 0 else 2
     vmem = pltpu.VMEM
     dma = pltpu.SemaphoreType.DMA
     volume, boundary = pl.pallas_call(
@@ -547,13 +533,13 @@
             vmem((2, slab_rows, width), BF16),
             vmem((128, nodes), BF16),
             vmem((comps * 8, nodes), BF16),
-            vmem((2, nodes * 2 // 3, cols * 8), BF16),
-            vmem((rows, nodes * 2 // 3, 256), BF16),
+            vmem((nodes // GROUPS, cols // GROUPS * 16), BF16),
+            vmem((rows, nodes * 2 // 3, 128), BF16),
             vmem((cols // GROUPS, GROUPS, 8, 128), BF16),
             vmem((GROUPS, cols // GROUPS, 8, 128), BF16),
-            vmem((cols // GROUPS, 8, 128), BF16),
-            vmem((rows, cols, 8, 128), BF16),
-            vmem((slab_rows, 128), F32),
+            vmem((GROUPS, pieces, group_half // pieces, 128), BF16),
+            vmem((rows, GROUPS, pieces, group_half // pieces, 128), BF16),
+            vmem((2, slab_rows, 128), F32),
             vmem((cols, 8, 128), BF16),
             vmem((cols, 8, 128), BF16),
             vmem((2, comps * 8, 128), BF16),
@@ -565,11 +551,11 @@
             vmem((2, 4, comps, 128), F32),
             vmem((4, comps, 128), F32),
             dma((6,)),
+            pltpu.SemaphoreType.REGULAR,
             dma(()),
             dma(()),
-            dma((6,)),
-            dma((6,)),
-            dma(()),
+            dma((3,)),
+            dma((3,)),
             dma((7, GROUPS)),
             dma((rows, GROUPS)),
             dma(()),

time: 38.4 us -> 36.3 us (0.945)
  Pallas kernels: 36.1 us -> 34 us
    pallas_call x1, Pallas kernels: 36.1 us -> 34 us  [on_device(): pl.pallas_call(functools.partial(kernel, rows, cols), out_shape=(pltpu.VM...]
where the time goes in v4:
time: 36.3 us; the launch traced here: 36.2 us
  Pallas kernels  34 us (94%)
  local copies, waits for them, and re-layouts  1.57 us (4%)
  between operations  0.64 us (2%)
    pallas_call x1, Pallas kernels, on_device(): pl.pallas_call(functools.partial(kernel, rows, cols), out_shape=(pltpu.VM...  34 us
    unnamed x2, local copies, waits for them, and re-layouts  1.57 us

profile of v4, /device:TPU:1, one launch (start us, length us, event | category | flops | bytes accessed | tf_op | source)
XLA Modules:
  0.0 36.2 jit_solution(13944963732333678158)
XLA Ops:
  0.6 34.0 %coupled_apply.1 = (f32[2048,128]{1,0:T(8,128)S(1)}, f32[16,64]{1,0:T(8,128)S(1)}) custom-call(f32[2048,128]{1,0:T(8,128)} %bitcast.7, f32[32,128]{1,0:T(8,128)} %bitcast.9, f32[64,1,384]{2,1,0:T(1,128)} %bitcast.8, s32[1,384]{1,0:T(1,128)} %bitcast.10, s32[1,32]{1,0:T(1,128)} %bitcast.11, bf16[2,512,3072]{2,1,0:T(8,128)(2,1)} %matrix_in.1), custom_call_target="tpu_custom_call" | custom-call | tf_op jit(solution)/shard_map/coupled_apply/pallas_call | solution.py:519
  34.6 1.0 %copy.10 = f32[64,4,8,128]{3,2,1,0:T(8,128)} copy(f32[64,4,8,128]{3,2,1,0:T(8,128)S(1)} %bitcast.6) | data formatting | bytes 2097152
  35.6 0.6 %copy.11 = f32[16,64]{1,0:T(8,128)} copy(f32[16,64]{1,0:T(8,128)S(1)} %get-tuple-element.7) | data formatting | bytes 8192

commit v5 on v4

--- a/solution.py
+++ b/solution.py
@@ -270,6 +270,7 @@
 
     for k, g in ((1, before), (2, after)):
         passed(k).wait_recv()
+        go(far_hops(g))
         go(first_hops(g))
 
     total[...] = jnp.zeros_like(total)
@@ -277,8 +278,6 @@
     passed(0).wait_recv()
     go(far_hops(across))
     go(first_hops(across))
-    go_on(before)
-    go_on(after)
 
     def face_copy(side):
         return remote(
@@ -322,7 +321,8 @@
 
     loads[5].wait()
     slab = matrix.shape[1]
-    window, shift = nodes * 2 // 3, nodes // 6
+    third = nodes // 3
+    early = mine // 2
     for late in range(2):
         part = (mine // 2 + late) % 2
 
@@ -332,33 +332,38 @@
         for step in steps + far_steps:
             if late:
                 arrivals(step, across)
+                arrivals(step, jnp.where(mine % 2 == 0, before, after))
+            else:
+                arrivals(step, jnp.where(mine % 2 == 0, after, before))
                 if step not in ((1, 0), (0, across_x)) or wide == 1:
-                    arrivals(step, jnp.where(mine % 2 == 0, before, after))
-            elif step not in ((1, 0), (0, across_x)) or wide == 1:
-                arrivals(step, mine)
-                arrivals(step, jnp.where(mine % 2 == 0, after, before))
+                    arrivals(step, mine)
 
         for r in range(rows):
             pieces = []
             for g in range(2):
                 block = traces[r, 2 * part + g].astype(F32).reshape(group_half, 2 * comps)
                 pieces += [block, pltpu.roll(block, comps, 1)]
-            placed[r, pl.ds(pl.multiple_of(part * shift, shift), nodes // 2), :] = jnp.concatenate(
-                pieces, axis=0
-            ).astype(BF16)
-            placed[r, pl.ds(pl.multiple_of((1 - part) * (nodes // 2), shift), shift), :] = (
-                jnp.zeros((shift, 128), BF16)
+            placed[r, pl.ds(pl.multiple_of(part * (nodes // 2), nodes // 2), nodes // 2), :] = (
+                jnp.concatenate(pieces, axis=0).astype(BF16)
             )
+
+        if late:
+            first, width, joined = (1 - early) * third, 2 * third, 1
+        else:
+            first, width, joined = 2 * early * third, third, 2
 
         @pl.loop(0, 2)
         def _(i):
             upright = pl.ds(pl.multiple_of(i * (slab // 2), slab // 2), slab // 2)
             for half in range(2):
                 terms = total[half, upright, :]
-                for r in range(rows):
-                    at = r * nodes + part * (nodes // 3)
-                    columns = pl.ds(pl.multiple_of(at, nodes // 3), window)
-                    terms += nn_dot(matrix[half, upright, columns], placed[r])
+                for r in range(0, rows, joined):
+                    lhs, rhs = [], []
+                    for q in range(r, r + joined):
+                        columns = pl.ds(pl.multiple_of(q * nodes + first, third), width)
+                        lhs.append(matrix[half, upright, columns])
+                        rhs.append(placed[q, pl.ds(pl.multiple_of(first, third), width), :])
+                    terms += nn_dot(jnp.concatenate(lhs, axis=1), jnp.concatenate(rhs, axis=0))
                 total[half, upright, :] = terms
 
     lower = iota((cols * 8, 128), 1) < comps
@@ -476,11 +481,11 @@
     for g in (mine, before, after, across):
         for copy in first_hops(g):
             copy.wait_send()
-    for g in (mine, before, after):
-        for copy in second_hops(g, 0, 3):
+    for copy in second_hops(mine, 0, 3):
+        copy.wait_send()
+    for g in (before, after, across):
+        for copy in far_hops(g):
             copy.wait_send()
-    for copy in far_hops(across):
-        copy.wait_send()
 
     for side in range(2):
 
@@ -534,7 +539,7 @@
             vmem((128, nodes), BF16),
             vmem((comps * 8, nodes), BF16),
             vmem((nodes // GROUPS, cols // GROUPS * 16), BF16),
-            vmem((rows, nodes * 2 // 3, 128), BF16),
+            vmem((rows, nodes, 128), BF16),
             vmem((cols // GROUPS, GROUPS, 8, 128), BF16),
             vmem((GROUPS, cols // GROUPS, 8, 128), BF16),
             vmem((GROUPS, pieces, group_half // pieces, 128), BF16),

time: 36.3 us -> 34.6 us (0.953)
  the two profiles are of different devices: /device:TPU:1 before, /device:TPU:33 now
where the time goes in v5:
time: 34.6 us; the launch traced here: 34.5 us
  Pallas kernels  32.3 us (93%)
  local copies, waits for them, and re-layouts  1.57 us (5%)
  between operations  0.64 us (2%)
    pallas_call x1, Pallas kernels, on_device(): pl.pallas_call(functools.partial(kernel, rows, cols), out_shape=(pltpu.VM...  32.3 us
    unnamed x2, local copies, waits for them, and re-layouts  1.57 us

profile of v5, /device:TPU:33, one launch (start us, length us, event | category | flops | bytes accessed | tf_op | source)
XLA Modules:
  0.0 34.5 jit_solution(8866076739318815235)
XLA Ops:
  0.6 32.3 %coupled_apply.1 = (f32[2048,128]{1,0:T(8,128)S(1)}, f32[16,64]{1,0:T(8,128)S(1)}) custom-call(f32[2048,128]{1,0:T(8,128)} %bitcast.7, f32[32,128]{1,0:T(8,128)} %bitcast.9, f32[64,1,384]{2,1,0:T(1,128)} %bitcast.8, s32[1,384]{1,0:T(1,128)} %bitcast.10, s32[1,32]{1,0:T(1,128)} %bitcast.11, bf16[2,512,3072]{2,1,0:T(8,128)(2,1)} %matrix_in.1), custom_call_target="tpu_custom_call" | custom-call | tf_op jit(solution)/shard_map/coupled_apply/pallas_call | solution.py:524
  32.9 1.0 %copy.10 = f32[64,4,8,128]{3,2,1,0:T(8,128)} copy(f32[64,4,8,128]{3,2,1,0:T(8,128)S(1)} %bitcast.6) | data formatting | bytes 2097152
  33.9 0.6 %copy.11 = f32[16,64]{1,0:T(8,128)} copy(f32[16,64]{1,0:T(8,128)S(1)} %get-tuple-element.7) | data formatting | bytes 8192

commit v6 on v5

--- a/solution.py
+++ b/solution.py
@@ -137,9 +137,8 @@
             slots.at[n], near.at[:, source], near_send, near_recv, me_r, mine * span + n
         )
 
-    @pl.loop(1, span)
-    def _(i):
-        near_copy((me_n + span - i) % span, me_n).start()
+    for step in sorted(range(1, span), key=lambda i: -min(i, span - i)):
+        near_copy((me_n + step) % span, me_n).start()
 
     own_slots = pltpu.make_async_copy(slots.at[me_n], near.at[:, me_n], near_recv)
     own_slots.start()
@@ -289,12 +288,6 @@
             me_c + 2 * side - 1,
         )
 
-    for side in range(2):
-
-        @pl.when(has[side])
-        def _():
-            face_copy(side).start()
-
     def corner_copy(side, way):
         return remote(
             edges_in.at[side, 3 * way],
@@ -337,6 +330,13 @@
                 arrivals(step, jnp.where(mine % 2 == 0, after, before))
                 if step not in ((1, 0), (0, across_x)) or wide == 1:
                     arrivals(step, mine)
+
+        if not late:
+            for side in range(2):
+
+                @pl.when(has[side])
+                def _():
+                    face_copy(side).start()
 
         for r in range(rows):
             pieces = []

time: 34.6 us -> 34 us (0.983)
  the two profiles are of different devices: /device:TPU:33 before, /device:TPU:1 now
where the time goes in v6:
time: 34 us; the launch traced here: 33.9 us
  Pallas kernels  31.7 us (93%)
  local copies, waits for them, and re-layouts  1.57 us (5%)
  between operations  0.64 us (2%)
    pallas_call x1, Pallas kernels, on_device(): pl.pallas_call(functools.partial(kernel, rows, cols), out_shape=(pltpu.VM...  31.7 us
    unnamed x2, local copies, waits for them, and re-layouts  1.57 us

profile of v6, /device:TPU:1, one launch (start us, length us, event | category | flops | bytes accessed | tf_op | source)
XLA Modules:
  0.0 33.9 jit_solution(3327809501206527522)
XLA Ops:
  0.6 31.7 %coupled_apply.1 = (f32[2048,128]{1,0:T(8,128)S(1)}, f32[16,64]{1,0:T(8,128)S(1)}) custom-call(f32[2048,128]{1,0:T(8,128)} %bitcast.7, f32[32,128]{1,0:T(8,128)} %bitcast.9, f32[64,1,384]{2,1,0:T(1,128)} %bitcast.8, s32[1,384]{1,0:T(1,128)} %bitcast.10, s32[1,32]{1,0:T(1,128)} %bitcast.11, bf16[2,512,3072]{2,1,0:T(8,128)(2,1)} %matrix_in.1), custom_call_target="tpu_custom_call" | custom-call | tf_op jit(solution)/shard_map/coupled_apply/pallas_call | solution.py:524
  32.3 1.0 %copy.10 = f32[64,4,8,128]{3,2,1,0:T(8,128)} copy(f32[64,4,8,128]{3,2,1,0:T(8,128)S(1)} %bitcast.6) | data formatting | bytes 2097152
  33.3 0.6 %copy.11 = f32[16,64]{1,0:T(8,128)} copy(f32[16,64]{1,0:T(8,128)S(1)} %get-tuple-element.7) | data formatting | bytes 8192

commit v7 on v6

--- a/solution.py
+++ b/solution.py
@@ -389,7 +389,7 @@
 
         @pl.loop(0, span)
         def _(i):
-            t = first + i
+            t = first + (me_n + span // 2 + i) % span
 
             @pl.when(t != me_c)
             def _():
@@ -447,7 +447,7 @@
         ring = 2.0 * (sides + depth_sides(u)) + outer
         return u, outer, ring, 4.0 * u + ring
 
-    @pl.loop(0, comps, unroll=4)
+    @pl.loop(0, comps, unroll=8)
     def _(k):
         layers = []
         for x in range(6):

time: 34 us -> 34 us (level)
  no operation moved by 1% of the time
where the time goes in v7:
time: 34 us; the launch traced here: 33.9 us
  Pallas kernels  31.7 us (93%)
  local copies, waits for them, and re-layouts  1.57 us (5%)
  between operations  0.64 us (2%)
    pallas_call x1, Pallas kernels, on_device(): pl.pallas_call(functools.partial(kernel, rows, cols), out_shape=(pltpu.VM...  31.7 us
    unnamed x2, local copies, waits for them, and re-layouts  1.57 us

profile of v7, /device:TPU:1, one launch (start us, length us, event | category | flops | bytes accessed | tf_op | source)
XLA Modules:
  0.0 33.9 jit_solution(2766652228822123533)
XLA Ops:
  0.6 31.7 %coupled_apply.1 = (f32[2048,128]{1,0:T(8,128)S(1)}, f32[16,64]{1,0:T(8,128)S(1)}) custom-call(f32[2048,128]{1,0:T(8,128)} %bitcast.7, f32[32,128]{1,0:T(8,128)} %bitcast.9, f32[64,1,384]{2,1,0:T(1,128)} %bitcast.8, s32[1,384]{1,0:T(1,128)} %bitcast.10, s32[1,32]{1,0:T(1,128)} %bitcast.11, bf16[2,512,3072]{2,1,0:T(8,128)(2,1)} %matrix_in.1), custom_call_target="tpu_custom_call" | custom-call | tf_op jit(solution)/shard_map/coupled_apply/pallas_call | solution.py:524
  32.3 1.0 %copy.10 = f32[64,4,8,128]{3,2,1,0:T(8,128)} copy(f32[64,4,8,128]{3,2,1,0:T(8,128)S(1)} %bitcast.6) | data formatting | bytes 2097152
  33.3 0.6 %copy.11 = f32[16,64]{1,0:T(8,128)} copy(f32[16,64]{1,0:T(8,128)S(1)} %get-tuple-element.7) | data formatting | bytes 8192
